TPU v7x, 256 devices: a whole 4x4x8 slice. The times are simulated.
256 devices in a mesh: tm: 8 (over y, x_hi), space: 32 (over z, x_lo, core).
Axes of the slice: x: 4 (x_hi: 2, x_lo: 2; x = x_hi * 2 + x_lo), y: 4, z: 8, core: 2. Of those that a mesh axis runs over, the one named last changes fastest.
Arguments:
- wave_field: bfloat16 [16, 8192, 256], P('tm', 'space'), may hold values from -600 to 600
- cotangent: bfloat16 [16, 8192, 256], P('tm', 'space'), may hold values from -6 to 6
- block_lists: int32 [16, 64, 4], P('tm', 'space'), may hold values from 0 to 63, as said below
- project_weights: bfloat16 [2, 256, 768], replicated, may hold values from -2 to 2
- combine_weights: bfloat16 [2, 256, 256], replicated, may hold values from -0.375 to 0.375
Outputs:
- mixed_field: bfloat16 [16, 8192, 256], P('tm', 'space')
- field_grad: bfloat16 [16, 8192, 256], P('tm', 'space')
- project_grad: float32 [2, 256, 768], replicated
- combine_grad: float32 [2, 256, 256], replicated
Inputs may be any that keep to these rules, and one draw needn't show every extreme that they name: `block_lists`: for frame f and block b, entry 0 is b itself, entry 1 is b - 2 or b + 2, and every entry lies within 2 blocks of b; entries may repeat.
All inputs are finite; a program needn't handle non-finite values.
Results may differ from a plain program's by a relative error of at most 0.012.
Values may be sent and summed in bfloat16 or wider, within the bound.
A program may use at most 128 MiB of HBM per device.

v0:
```python
import math

import jax
import jax.numpy as jnp
from jax import lax
from jax.sharding import PartitionSpec as P

HEADS = 8
BLOCK = 128
HREACH = 2


epsilon = 1e-05


def with_halo(cells, sides, width):
    for axis, dim in sides:
        count = lax.axis_size(axis)
        ends = count - 1
        head = lax.slice_in_dim(cells, 0, width, axis=dim)
        tail = lax.slice_in_dim(cells, cells.shape[dim] - width, cells.shape[dim], axis=dim)
        cells = jnp.concatenate(
            [
                lax.ppermute(tail, axis, [(i, (i + 1) % count) for i in range(ends)]),
                cells,
                lax.ppermute(head, axis, [((i + 1) % count, i) for i in range(ends)]),
            ],
            axis=dim,
        )
    return cells


def layer_norm(tok_rows):
    widened = tok_rows.astype(jnp.float32)
    centered = widened - jnp.mean(widened, axis=-1, keepdims=True)
    inverse = lax.rsqrt(jnp.mean(centered * centered, axis=-1, keepdims=True) + epsilon)
    return (centered * inverse, inverse)


def norm_backward(upstream, normed, inverse):
    mean_grad = jnp.mean(upstream, axis=-1, keepdims=True)
    mean_cross = jnp.mean(upstream * normed, axis=-1, keepdims=True)
    return inverse * (upstream - mean_grad - normed * mean_cross)


def matmul(left_op, right_op):
    return jnp.dot(left_op, right_op, preferred_element_type=jnp.float32)


def wide_dot(left_op, right_op):
    return jnp.dot(
        left_op.astype(jnp.float32), right_op.astype(jnp.float32), precision=lax.Precision.HIGHEST
    )


def matmul_left(left_op, right_op):
    return lax.dot_general(
        left_op, right_op, (((0,), (0,)), ((), ())), preferred_element_type=jnp.float32
    )


def matmul_right(left_op, right_op):
    return lax.dot_general(
        left_op, right_op, (((1,), (1,)), ((), ())), preferred_element_type=jnp.float32
    )


def einsum_wide(formula, left_op, right_op):
    return jnp.einsum(formula, left_op, right_op, preferred_element_type=jnp.float32)


def softmax_rows(scores, reduce_axis):
    row_max = jnp.max(scores, axis=reduce_axis, keepdims=True)
    exp_scores = jnp.exp(scores - row_max)
    return lax.optimization_barrier(
        (exp_scores / jnp.sum(exp_scores, axis=reduce_axis, keepdims=True)).astype(jnp.bfloat16)
    )


def temporal_pair(tok_rows, cot_rows, project, combine, score_scale):
    frame_count, row_count, features = tok_rows.shape
    head_width = features // HEADS
    normed, inverse = layer_norm(tok_rows)
    normed_act = normed.astype(jnp.bfloat16).reshape(frame_count * row_count, features)
    projected = (
        matmul(normed_act, project)
        .astype(jnp.bfloat16)
        .reshape(frame_count, row_count, 3, HEADS, head_width)
    )
    queries = projected[:, :, 0]
    key_part = projected[:, :, 1]
    value_part = projected[:, :, 2]
    attn_probs = softmax_rows(einsum_wide("frhe,grhe->hfgr", queries, key_part) * score_scale, 2)
    attended = (
        einsum_wide("hfgr,grhe->frhe", attn_probs, value_part)
        .astype(jnp.bfloat16)
        .reshape(frame_count * row_count, features)
    )
    mixed = (
        tok_rows.astype(jnp.float32)
        + matmul(attended, combine).reshape(frame_count, row_count, features)
    ).astype(jnp.bfloat16)
    flat_cot = cot_rows.reshape(frame_count * row_count, features)
    outward = matmul_left(attended, flat_cot)
    attn_grad = (
        matmul_right(flat_cot, combine)
        .astype(jnp.bfloat16)
        .reshape(frame_count, row_count, HEADS, head_width)
    )
    grad_probs = einsum_wide("frhe,grhe->hfgr", attn_grad, value_part)
    prob_wide = attn_probs.astype(jnp.float32)
    row_delta = jnp.sum(prob_wide * grad_probs, axis=2, keepdims=True)
    grad_scores = (prob_wide * (grad_probs - row_delta) * score_scale).astype(jnp.bfloat16)
    grad_query = einsum_wide("hfgr,grhe->frhe", grad_scores, key_part)
    grad_keys = einsum_wide("hfgr,frhe->grhe", grad_scores, queries)
    grad_values = einsum_wide("hfgr,frhe->grhe", attn_probs, attn_grad)
    project_rows = (
        jnp.stack([grad_query, grad_keys, grad_values], axis=2)
        .astype(jnp.bfloat16)
        .reshape(frame_count * row_count, 3 * features)
    )
    inward = matmul_left(normed_act, project_rows)
    act_grad = matmul_right(project_rows, project).reshape(frame_count, row_count, features)
    field_rows = (cot_rows.astype(jnp.float32) + norm_backward(act_grad, normed, inverse)).astype(
        jnp.bfloat16
    )
    return (mixed, field_rows, inward, outward)


def owner_sums(tile_sums, edge_sums, rim_rows, row_count):
    arrived = with_halo(edge_sums.astype(jnp.bfloat16), (("space", 1),), rim_rows).astype(
        edge_sums.dtype
    )
    pair_grad = tile_sums[:, rim_rows : rim_rows + row_count]
    pair_grad = pair_grad + arrived[:, :rim_rows]
    pair_grad = pair_grad + arrived[:, 3 * rim_rows :]
    return pair_grad


def per_device(wave_field, cotangent, block_lists, project_weights, combine_weights):
    frame_count, row_count, features = wave_field.shape
    head_width = features // HEADS
    score_scale = 1.0 / math.sqrt(head_width)
    block_count = row_count // BLOCK
    list_length = block_lists.shape[-1]
    rim_rows = HREACH * BLOCK
    padded_blocks = block_count + 2 * HREACH
    group_count = frame_count * block_count // 4
    space_project = project_weights[0]
    space_combine = combine_weights[0]
    normed, inverse = layer_norm(wave_field)
    normed_act = normed.astype(jnp.bfloat16)
    flat_act = normed_act.reshape(frame_count * row_count, features)
    projected = (
        matmul(flat_act, space_project)
        .astype(jnp.bfloat16)
        .reshape(frame_count, row_count, 3 * features)
    )
    keys_values = projected[:, :, features:]
    extended = with_halo(keys_values, (("space", 1),), rim_rows)
    first_block = lax.axis_index("space") * block_count - HREACH
    frame_base = (jnp.arange(frame_count, dtype=jnp.int32) * padded_blocks)[:, None, None]
    group_index = (block_lists - first_block + frame_base).reshape(group_count, 4 * list_length)
    padded_flat = extended.reshape(frame_count * padded_blocks, BLOCK, 2, HEADS, head_width)
    queries = projected[:, :, :features].reshape(group_count, 4, BLOCK, HEADS, head_width)

    def group_weights(group_query, group_rows):
        picked = jnp.take(padded_flat, group_rows, axis=0).reshape(
            4, list_length * BLOCK, 2, HEADS, head_width
        )
        scores = einsum_wide("gqhe,gkhe->ghqk", group_query, picked[:, :, 0]) * score_scale
        return (picked, softmax_rows(scores, 3))

    def forward_group(element):
        picked, attn_probs = group_weights(element[0], element[1])
        return einsum_wide("ghqk,gkhe->gqhe", attn_probs, picked[:, :, 1]).astype(jnp.bfloat16)

    attended = lax.map(forward_group, (queries, group_index)).reshape(
        frame_count * row_count, features
    )
    mixed_space = (
        wave_field.astype(jnp.float32)
        + matmul(attended, space_combine).reshape(frame_count, row_count, features)
    ).astype(jnp.bfloat16)
    history, history_cot = (
        lax.all_to_all(mixed_space, "tm", split_axis=1, concat_axis=0, tiled=True),
        lax.all_to_all(cotangent, "tm", split_axis=1, concat_axis=0, tiled=True),
    )
    time_mixed, time_grad, time_inward, time_outward = temporal_pair(
        history, history_cot, project_weights[1], combine_weights[1], score_scale
    )
    mixed_field, mixed_grad = (
        lax.all_to_all(time_mixed, "tm", split_axis=0, concat_axis=1, tiled=True),
        lax.all_to_all(time_grad, "tm", split_axis=0, concat_axis=1, tiled=True),
    )
    flat_grad = mixed_grad.reshape(frame_count * row_count, features)
    space_outward = matmul_left(attended, flat_grad)
    attn_grad = (
        matmul_right(flat_grad, space_combine)
        .astype(jnp.bfloat16)
        .reshape(group_count, 4, BLOCK, HEADS, head_width)
    )

    def backward_group(running, element):
        group_query, group_rows, group_grad = element
        picked, attn_probs = group_weights(group_query, group_rows)
        key_part = picked[:, :, 0]
        value_part = picked[:, :, 1]
        prob_wide = attn_probs.astype(jnp.float32)
        grad_probs = einsum_wide("gqhe,gkhe->ghqk", group_grad, value_part)
        row_delta = jnp.sum(prob_wide * grad_probs, axis=3, keepdims=True)
        grad_scores = (prob_wide * (grad_probs - row_delta) * score_scale).astype(jnp.bfloat16)
        grad_query = einsum_wide("ghqk,gkhe->gqhe", grad_scores, key_part).astype(jnp.bfloat16)
        grad_keys = einsum_wide("ghqk,gqhe->gkhe", grad_scores, group_query)
        grad_values = einsum_wide("ghqk,gqhe->gkhe", attn_probs, group_grad)
        key_tiles = jnp.stack([grad_keys, grad_values], axis=2).reshape(
            4 * list_length, BLOCK * 2 * features
        )
        return (running.at[group_rows].add(key_tiles), grad_query)

    zero_tiles = jnp.zeros((frame_count * padded_blocks, BLOCK * 2 * features), jnp.float32)
    tile_sums, grad_query = lax.scan(backward_group, zero_tiles, (queries, group_index, attn_grad))
    tile_sums = tile_sums.reshape(frame_count, row_count + 2 * rim_rows, 2 * features)
    edge_sums = jnp.concatenate(
        [tile_sums[:, :rim_rows], tile_sums[:, rim_rows + row_count :]], axis=1
    )
    kv_project = space_project[:, features:]
    query_flat = grad_query.reshape(frame_count * row_count, features)
    pair_grad = owner_sums(tile_sums, edge_sums, rim_rows, row_count)
    pair_flat = pair_grad.reshape(frame_count * row_count, 2 * features)
    space_inward = jnp.concatenate(
        [matmul_left(flat_act, query_flat), wide_dot(flat_act.T, pair_flat)], axis=1
    )
    act_grad = matmul_right(query_flat, space_project[:, :features]) + wide_dot(
        pair_flat, kv_project.T
    )
    act_grad = act_grad.reshape(frame_count, row_count, features)
    field_grad = (mixed_grad.astype(jnp.float32) + norm_backward(act_grad, normed, inverse)).astype(
        jnp.bfloat16
    )
    space_inward, space_outward, time_inward, time_outward = lax.psum(
        (space_inward, space_outward, time_inward, time_outward), ("tm", "space")
    )
    factor = 1.0 / math.sqrt(frame_count * row_count * lax.axis_size("tm") * lax.axis_size("space"))
    project_grad = jnp.stack([space_inward, time_inward]) * factor
    combine_grad = jnp.stack([space_outward, time_outward]) * factor
    return (mixed_field, field_grad, project_grad, combine_grad)


def solution(mesh):
    in_specs = (P("tm", "space", None), P("tm", "space", None), P("tm", "space", None), P(), P())
    out_specs = (P("tm", "space", None), P("tm", "space", None), P(), P())
    return jax.shard_map(
        per_device, mesh=mesh, in_specs=in_specs, out_specs=out_specs, check_vma=False
    )
```

profile of v0, /device:TPU:1, one launch (start us, length us, event | category | flops | bytes accessed | tf_op | source)
XLA Modules:
  0.0 561.6 jit_solution(7572471238798868176)
XLA Ops:
  13.4 5.1 collective-permute-start.1
  21.4 6.0 %all-to-all-start.2 = ((bf16[2,256,256]{2,0,1:T(2,128)(2,1)}), bf16[2,256,256]{2,0,1:T(2,128)(2,1)S(1)}, u32[]{:S(2)}, u32[]{:S(2)}) async-start(bf16[2,256,256]{2,0,1:T(2,128)(2,1)} %copy.163), calls=%async_computation.2 | async-start | bytes 524288 | tf_op jit(solution)/shard_map/all_to_all | solution.py:187
  28.9 9.8 %all-to-all-done.2 = bf16[2,256,256]{2,0,1:T(2,128)(2,1)S(1)} async-done(((bf16[2,256,256]{2,0,1:T(2,128)(2,1)}), bf16[2,256,256]{2,0,1:T(2,128)(2,1)S(1)}, u32[]{:S(2)}, u32[]{:S(2)}) %all-to-all-start.2) | async-done | bytes 262176 | tf_op jit(solution)/shard_map/all_to_all | solution.py:187
  38.7 3.1 pad_maximum_fusion.2
  58.4 6.7 %fusion.100 = (f32[4,8,128]{2,1,0:T(8,128)S(1)}, f32[4,8,128,512]{3,2,1,0:T(8,128)S(1)}) fusion(f32[4,8,128,512]{3,2,1,0:T(8,128)S(1)} %fusion.42), kind=kOutput, calls=%fused_computation.168 | output fusion | flops 8389119 | bytes 16793600 | tf_op jit(solution)/shard_map/while/body/eval_jaxpr/sub | solution.py:74
  71.1 3.7 all-to-all-start
  76.4 7.3 %all-to-all-done = bf16[2,256,256]{2,0,1:T(2,128)(2,1)S(1)} async-done(((bf16[2,256,256]{2,0,1:T(2,128)(2,1)}), bf16[2,256,256]{2,0,1:T(2,128)(2,1)S(1)}, u32[]{:S(2)}, u32[]{:S(2)}) %all-to-all-start) | async-done | bytes 262176 | tf_op jit(solution)/shard_map/all_to_all | solution.py:186
  87.3 3.6 reshape.240
  93.6 3.7 fusion.37
  97.3 3.3 divide_convert_fusion.1
  110.3 11.7 %fusion.24 = bf16[16,32,1,8,32]{4,0,3,1,2:T(8,128)(2,1)S(1)} fusion(bf16[16,32,8,32]{3,2,1,0:T(8,128)(2,1)S(1)} %copy-done.8, bf16[8,16,16,32]{1,2,3,0:T(8,128)(2,1)S(1)} %fusion.15), kind=kOutput, calls=%fused_computation.45 | convolution fusion | flops 4325376 | bytes 655360 | tf_op jit(solution)/shard_map/hfgr,grhe->frhe/dot_general | solution.py:69
  136.8 3.4 all-to-all-start.3
  142.0 6.6 %all-to-all-done.3 = bf16[16,32,256]{2,1,0:T(8,128)(2,1)S(1)} async-done(((bf16[16,32,256]{2,1,0:T(8,128)(2,1)}), bf16[16,32,256]{2,1,0:T(8,128)(2,1)S(1)}, u32[]{:S(2)}, u32[]{:S(2)}) %all-to-all-start.3) | async-done | bytes 262176 | tf_op jit(solution)/shard_map/all_to_all | solution.py:194
  148.6 4.0 all-to-all-start.1
  153.9 3.0 convolution_bitcast_fusion
  156.9 4.5 fusion.41
  161.4 11.7 %fusion.21 = f32[4,512,1,8,32]{1,4,3,0,2:T(8,128)} fusion(bf16[4,8,128,512]{3,2,1,0:T(8,128)(2,1)} %copy-done, f32[4,8,128,512]{3,2,1,0:T(8,128)} %fusion.41, bf16[4,128,8,32]{1,0,3,2:T(4,128)(2,1)S(1)} %copy-done.26), kind=kOutput, calls=%fused_computation.33 | convolution fusion | flops 148902400 | bytes 14942208 | tf_op jit(solution)/shard_map/while/body/eval_jaxpr/ghqk,gqhe->gkhe/dot_general | solution.py:69
  173.1 4.1 pad_maximum_fusion
  177.3 12.6 %copy.182 = f32[4,512,2,8,32]{4,3,2,1,0:T(8,128)} copy(f32[4,512,2,8,32]{1,4,3,0,2:T(8,128)} %pad_maximum_fusion) | data formatting | bytes 8388608 | tf_op jit(solution)/shard_map/while/body/eval_jaxpr/stack | solution.py:216
  189.9 16.9 %reshape.268 = f32[16,65536]{1,0:T(8,128)} reshape(f32[4,512,2,8,32]{4,3,2,1,0:T(8,128)} %copy.182) | data formatting | bytes 8388608 | tf_op jit(solution)/shard_map/while/body/eval_jaxpr/reshape | solution.py:216
  209.0 38.2 %scatter_fusion = f32[12,65536]{1,0:T(8,128)} fusion(f32[12,65536]{1,0:T(8,128)} %broadcast_in_dim.24, s32[16]{0:T(128)S(1)} %fusion.91, f32[16,65536]{1,0:T(8,128)} %reshape.268), kind=kCustom, calls=%fused_computation.1 | custom fusion | flops 1048576 | bytes 12582976 | tf_op jit(solution)/shard_map/while/body/eval_jaxpr/scatter-add | solution.py:219
  251.3 11.5 %fusion.31 = bf16[4,128,8,32]{1,3,2,0:T(8,128)(2,1)} fusion(bf16[4,8,128,512]{3,2,1,0:T(8,128)(2,1)} %copy-done, f32[4,8,128,512]{3,2,1,0:T(8,128)} %fusion.41, bf16[4,512,1,8,32]{1,0,4,3,2:T(4,128)(2,1)} %copy-done.6), kind=kOutput, calls=%fused_computation.62 | convolution fusion | flops 149033472 | bytes 13893632 | tf_op jit(solution)/shard_map/while/body/eval_jaxpr/ghqk,gkhe->gqhe/dot_general | solution.py:69
  264.9 3.2 collective-permute-start.3
  283.0 267.8 %all-reduce.3.cloned.1.call-done = (f32[1,256,768]{2,1,0:T(8,128)}, f32[1,256,768]{2,1,0:T(8,128)}, f32[1,256,256]{2,1,0:T(8,128)}, f32[1,256,256]{2,1,0:T(8,128)}) async-done(((f32[1,256,768]{2,1,0:T(8,128)}, f32[1,256,768]{2,1,0:T(8,128)}, f32[1,256,256]{2,1,0:T(8,128)}, f32[1,256,256]{2,1,0:T(8,128)}), (f32[1,256,768]{2,1,0:T(8,128)}, f32[1,256,768]{2,1,0:T(8,128)}, f32[1,256,256]{2,1,0:T(8,128)}, ...) | async-done | bytes 2097168 | tf_op jit(solution)/shard_map/psum | solution.py:241
  (172 shorter events, 94.8 us)
Async XLA Ops:
  7.2 20.2 %copy-start.18 = (bf16[2,256,768]{2,1,0:T(8,128)(2,1)S(1)}, bf16[2,256,768]{2,1,0:T(8,128)(2,1)}, u32[]{:S(2)}) copy-start(bf16[2,256,768]{2,1,0:T(8,128)(2,1)} %param.10) | copy-start | bytes 2359300
  7.2 13.2 %copy-start.31 = (bf16[2,256,256]{2,1,0:T(8,128)(2,1)S(1)}, bf16[2,256,256]{2,1,0:T(8,128)(2,1)}, u32[]{:S(2)}) copy-start(bf16[2,256,256]{2,1,0:T(8,128)(2,1)} %param.8) | copy-start | bytes 786436
  8.4 19.8 %copy-start.34 = (s32[2,2,4]{2,1,0:T(2,128)S(1)}, s32[2,2,4]{2,1,0:T(2,128)}, u32[]{:S(2)}) copy-start(s32[2,2,4]{2,1,0:T(2,128)} %param.9) | copy-start | bytes 196
  13.4 25.3 %collective-permute-start.1 = (bf16[2,256,512]{1,0,2:T(2,128)(2,1)S(1)}, bf16[2,256,512]{1,0,2:T(2,128)(2,1)}, u32[]{:S(2)}, u32[]{:S(2)}) collective-permute-start(bf16[2,256,512]{1,0,2:T(2,128)(2,1)S(1)} %copy.194), channel_id=1, source_target_pairs={{1,0},{2,1},{3,2},{4,3},{5,4},{6,5},{7,6},{8,7},{9,8},{10,9},{11,1... | collective-permute-start | bytes 1572872 | tf_op jit(solution)/shard_map/ppermute | solution.py:26
  18.5 20.2 %collective-permute-start = (bf16[2,256,512]{1,0,2:T(2,128)(2,1)S(1)}, bf16[2,256,512]{1,0,2:T(2,128)(2,1)}, u32[]{:S(2)}, u32[]{:S(2)}) collective-permute-start(bf16[2,256,512]{1,0,2:T(2,128)(2,1)S(1)} %copy.194), channel_id=1, source_target_pairs={{0,1},{1,2},{2,3},{3,4},{4,5},{5,6},{6,7},{7,8},{8,9},{9,10},{10,1... | collective-permute-start | bytes 1572872 | tf_op jit(solution)/shard_map/ppermute | solution.py:24
  21.4 17.3 %all-to-all-start.2 = ((bf16[2,256,256]{2,0,1:T(2,128)(2,1)}), bf16[2,256,256]{2,0,1:T(2,128)(2,1)S(1)}, u32[]{:S(2)}, u32[]{:S(2)}) async-start(bf16[2,256,256]{2,0,1:T(2,128)(2,1)} %copy.163), calls=%async_computation.2 | async-start | bytes 524288 | tf_op jit(solution)/shard_map/all_to_all | solution.py:187
  28.8 27.3 %copy-start.25 = (bf16[4,128,8,32]{1,0,3,2:T(4,128)(2,1)}, bf16[4,128,8,32]{1,0,3,2:T(4,128)(2,1)S(1)}, u32[]{:S(2)}) copy-start(bf16[4,128,8,32]{1,0,3,2:T(4,128)(2,1)S(1)} %squeeze.57) | copy-start | bytes 786436
  38.7 36.1 %copy-start.11 = (bf16[2,8,32,256]{3,2,0,1:T(8,128)(2,1)}, bf16[2,8,32,256]{3,2,0,1:T(8,128)(2,1)S(1)}, u32[]{:S(2)}) copy-start(bf16[2,8,32,256]{3,2,0,1:T(8,128)(2,1)S(1)} %copy.164) | copy-start | bytes 786436
  56.1 9.8 %copy-start.1 = (bf16[4,512,1,8,32]{1,0,4,3,2:T(4,128)(2,1)}, bf16[4,512,1,8,32]{1,0,4,3,2:T(4,128)(2,1)S(1)}, u32[]{:S(2)}) copy-start(bf16[4,512,1,8,32]{1,0,4,3,2:T(4,128)(2,1)S(1)} %get-tuple-element.53) | copy-start | bytes 3145732
  69.6 15.7 %copy-start.22 = (bf16[4,128,8,32]{1,0,3,2:T(4,128)(2,1)}, bf16[4,128,8,32]{1,0,3,2:T(4,128)(2,1)S(1)}, u32[]{:S(2)}) copy-start(bf16[4,128,8,32]{1,0,3,2:T(4,128)(2,1)S(1)} %copy.151) | copy-start | bytes 786436
  69.8 16.2 %copy-start.19 = (bf16[2,256,768]{2,1,0:T(8,128)(2,1)S(1)}, bf16[2,256,768]{2,1,0:T(8,128)(2,1)}, u32[]{:S(2)}) copy-start(bf16[2,256,768]{2,1,0:T(8,128)(2,1)} %param.10) | copy-start | bytes 2359300
  71.1 12.7 %all-to-all-start = ((bf16[2,256,256]{2,0,1:T(2,128)(2,1)}), bf16[2,256,256]{2,0,1:T(2,128)(2,1)S(1)}, u32[]{:S(2)}, u32[]{:S(2)}) async-start(bf16[2,256,256]{2,0,1:T(2,128)(2,1)} %copy.153), calls=%async_computation | async-start | bytes 524288 | tf_op jit(solution)/shard_map/all_to_all | solution.py:186
  129.2 6.0 %copy-start.20 = (bf16[2,256,768]{2,1,0:T(8,128)(2,1)S(1)}, bf16[2,256,768]{2,1,0:T(8,128)(2,1)}, u32[]{:S(2)}) copy-start(bf16[2,256,768]{2,1,0:T(8,128)(2,1)} %param.10) | copy-start | bytes 2359300
  129.2 6.0 %copy-start.21 = (bf16[16,32,768]{2,1,0:T(8,128)(2,1)S(1)}, bf16[16,32,768]{2,1,0:T(8,128)(2,1)}, u32[]{:S(2)}) copy-start(bf16[16,32,768]{2,1,0:T(8,128)(2,1)} %convert_element_type.167) | copy-start | bytes 2359300
  130.4 5.3 copy-start.12
  135.0 5.2 copy-start.28
  135.7 17.8 %copy-start.30 = (bf16[2,256,256]{2,1,0:T(8,128)(2,1)S(1)}, bf16[2,256,256]{2,1,0:T(8,128)(2,1)}, u32[]{:S(2)}) copy-start(bf16[2,256,256]{2,1,0:T(8,128)(2,1)} %param.11) | copy-start | bytes 786436
  136.8 11.8 %all-to-all-start.3 = ((bf16[16,32,256]{2,1,0:T(8,128)(2,1)}), bf16[16,32,256]{2,1,0:T(8,128)(2,1)S(1)}, u32[]{:S(2)}, u32[]{:S(2)}) async-start(bf16[16,32,256]{2,1,0:T(8,128)(2,1)} %fusion.58), calls=%async_computation.3 | async-start | bytes 524288 | tf_op jit(solution)/shard_map/all_to_all | solution.py:194
  148.6 121.5 %all-to-all-start.1 = ((bf16[16,32,256]{2,1,0:T(8,128)(2,1)}), bf16[16,32,256]{2,1,0:T(8,128)(2,1)}, u32[]{:S(2)}, u32[]{:S(2)}) async-start(bf16[16,32,256]{2,1,0:T(8,128)(2,1)} %fusion.29), calls=%async_computation.1 | async-start | bytes 524288 | tf_op jit(solution)/shard_map/all_to_all | solution.py:193
  152.7 398.1 %all-reduce.3.cloned.1.call-start = ((), (), s32[]{:S(2)}) async-start(), calls=%async_computation.4 | async-start | bytes 4194304 | tf_op jit(solution)/shard_map/psum | solution.py:241
  156.9 4.5 copy-start.26
  262.8 13.4 %collective-permute-start.2 = (bf16[2,256,512]{2,1,0:T(8,128)(2,1)}, bf16[2,256,512]{2,1,0:T(8,128)(2,1)}, u32[]{:S(2)}, u32[]{:S(2)}) collective-permute-start(bf16[2,256,512]{2,1,0:T(8,128)(2,1)} %get-tuple-element.55), channel_id=1, source_target_pairs={{0,1},{1,2},{2,3},{3,4},{4,5},{5,6},{6,7},{7,8},{8,9},{9,10},{10,1... | collective-permute-start | bytes 1572872 | tf_op jit(solution)/shard_map/ppermute | solution.py:24
  264.9 11.3 %collective-permute-start.3 = (bf16[2,256,512]{2,1,0:T(8,128)(2,1)}, bf16[2,256,512]{2,1,0:T(8,128)(2,1)}, u32[]{:S(2)}, u32[]{:S(2)}) collective-permute-start(bf16[2,256,512]{2,1,0:T(8,128)(2,1)} %get-tuple-element.56), channel_id=1, source_target_pairs={{1,0},{2,1},{3,2},{4,3},{5,4},{6,5},{7,6},{8,7},{9,8},{10,9},{11,1... | collective-permute-start | bytes 1572872 | tf_op jit(solution)/shard_map/ppermute | solution.py:26
  271.8 6.8 %copy-start.16 = (bf16[2,256,256]{2,1,0:T(8,128)(2,1)S(1)}, bf16[2,256,256]{2,1,0:T(8,128)(2,1)}, u32[]{:S(2)}) copy-start(bf16[2,256,256]{2,1,0:T(8,128)(2,1)} %copy-done.15) | copy-start | bytes 786436
  (20 other events, 36.9 us)
Sparse Core Ops, SparseCore 0:
  280.4 270.3 all-reduce.2
where the time goes:
time: 571 us; the launch traced here: 562 us
  waiting for transfers between devices  292 us (51%)
  local copies, waits for them, and re-layouts  81.3 us (14%)
  other arithmetic  73.4 us (13%)
  matrix products  70.6 us (12%)
  starting transfers between devices  29.6 us (5%)
  between operations  15.3 us (3%)
    psum x1, waiting for transfers between devices, per_device(): lax.psum((space_inward, space_outward, time_inward, time_outward), ('tm',...  268 us
    dot_general x12, matrix products, einsum_wide(): jnp.einsum(formula, left_op, right_op, preferred_element_type=jnp.float32)  53.7 us
    scatter-add x1, other arithmetic, backward_group(): return (running.at[group_rows].add(key_tiles), grad_query)  38.2 us
    reshape x1, local copies, waits for them, and re-layouts, backward_group(): jnp.stack([grad_keys, grad_values], axis=2)  16.9 us
    another operation x1, local copies, waits for them, and re-layouts, backward_group(): jnp.stack([grad_keys, grad_values], axis=2)  12.6 us
  transfers between devices with their start and end apart: 9, of which 4 were waited for; matrix products, arithmetic and copies ran while one was open for 22% of the time, Pallas kernels for 0%

commit v1 on v0

v1 whole, which is shorter than its diff:
```python
import functools
import math

import jax
import jax.numpy as jnp
from jax import lax
from jax.experimental import pallas as pl
from jax.experimental.pallas import tpu as pltpu
from jax.sharding import PartitionSpec as P

HEADS = 8
BLOCK = 128
SPAN = 5
KEYS = SPAN * BLOCK
D = 256
HD = 32
ROWS = 256
FR = 2
GROUPS = 4
CORES = 4
EPS = 1e-05
NEG = -1e30
SCALE = 1.0 / math.sqrt(HD)
SCALE2 = SCALE * math.log2(math.e)

MESH = pl.DeviceIdType.MESH
F32 = jnp.float32
BF16 = jnp.bfloat16


def nn(left, right):
    return jnp.dot(left, right, preferred_element_type=F32)


def nt(left, right):
    return lax.dot_general(left, right, (((1,), (1,)), ((), ())), preferred_element_type=F32)


def norm(rows):
    centered = rows - jnp.mean(rows, axis=-1, keepdims=True)
    inverse = lax.rsqrt(jnp.mean(centered * centered, axis=-1, keepdims=True) + EPS)
    return centered * inverse, inverse


def norm_back(upstream, normed, inverse):
    mean_grad = jnp.mean(upstream, axis=-1, keepdims=True)
    mean_cross = jnp.mean(upstream * normed, axis=-1, keepdims=True)
    return inverse * (upstream - mean_grad - normed * mean_cross)


def diag(pair):
    return jnp.concatenate([pair[0:HD, 0:BLOCK], pair[HD : 2 * HD, BLOCK : 2 * BLOCK]], axis=0)


def head_sums(prod):
    return jnp.sum(prod.reshape(HEADS, HD, BLOCK), axis=1)


def scratch_shapes(ntm, nsp):
    nz = nsp // CORES
    npl = ntm * CORES
    part = ROWS // ntm
    chunk = 512 // npl
    dma = pltpu.SemaphoreType.DMA
    vm = pltpu.VMEM
    return dict(
        xe=vm((3, FR, ROWS, D), BF16),
        act=vm((3, FR, ROWS, D), BF16),
        act_t=vm((FR, D, 3 * ROWS), BF16),
        nrm=vm((FR, ROWS, D), F32),
        rinv=vm((FR, ROWS, 1), F32),
        wv=vm((2, D, 3 * D), BF16),
        cv=vm((2, D, D), BF16),
        wt=vm((2, 2 * D, D), BF16),
        hm=vm((HEADS, BLOCK, D), BF16),
        q=vm((FR, ROWS, D), BF16),
        kv=vm((FR, 3 * ROWS, 2 * D), BF16),
        kvt=vm((FR, 2 * D, 3 * ROWS), BF16),
        qs=vm((4, HEADS * BLOCK, D), BF16),
        dos=vm((HEADS * BLOCK, D), BF16),
        probs=vm((4, KEYS, HEADS * BLOCK), BF16),
        ds=vm((KEYS, HEADS * BLOCK), BF16),
        s=vm((2, KEYS, 2 * BLOCK), F32),
        ot=vm((4, D, BLOCK), F32),
        otb=vm((D, 4 * BLOCK), BF16),
        att=vm((FR, ROWS, D), BF16),
        ms=vm((FR, ROWS, D), BF16),
        hist=vm((ntm, FR, part, D), BF16),
        hcot=vm((ntm, FR, part, D), BF16),
        xt=vm((GROUPS, BLOCK, D), F32),
        ct=vm((GROUPS, BLOCK, D), F32),
        tb=vm((BLOCK, 2 * BLOCK), F32),
        tnrm=vm((GROUPS * BLOCK, D), F32),
        trinv=vm((GROUPS * BLOCK, 1), F32),
        tact=vm((GROUPS * BLOCK, D), BF16),
        tp=vm((GROUPS * BLOCK, 3 * D), BF16),
        tkvt=vm((2 * D, GROUPS * BLOCK), BF16),
        tdo=vm((GROUPS * BLOCK, D), BF16),
        tdot=vm((D, GROUPS * BLOCK), BF16),
        tot=vm((D, GROUPS * BLOCK), BF16),
        tatt=vm((GROUPS * BLOCK, D), BF16),
        tdp=vm((GROUPS * BLOCK, 3 * D), BF16),
        tqs=vm((HEADS * BLOCK, D), BF16),
        tmix=vm((GROUPS, BLOCK, D), F32),
        mfs=vm((ntm, FR, part, D), BF16),
        mgs=vm((ntm, FR, part, D), BF16),
        mg=vm((FR, ROWS, D), BF16),
        do=vm((FR, ROWS, D), BF16),
        dot_t=vm((D, FR * ROWS), BF16),
        dq=vm((FR, ROWS, D), BF16),
        dkv=vm((FR, 3 * ROWS, 2 * D), F32),
        dkvb=vm((FR, 3 * ROWS, 2 * D), BF16),
        er=vm((FR, 2, ROWS, 2 * D), BF16),
        g=vm((2, 512, 512), BF16),
        rs=vm((2, npl - 1, chunk, 512), BF16),
        zb=vm((2, nz, chunk, 512), BF16),
        fin=vm((2, 512, 512), BF16),
        ld_sem=dma((6,)),
        halo_s=dma((2,)),
        halo_r=dma((2,)),
        cot_s=dma((ntm - 1,)),
        cot_r=dma((ntm - 1,)),
        ms_s=dma((FR, ntm - 1)),
        ms_r=dma((FR, ntm - 1)),
        mf_s=dma((ntm - 1,)),
        mf_r=dma((ntm - 1,)),
        mg_s=dma((ntm - 1,)),
        mg_r=dma((ntm - 1,)),
        ed_s=dma((FR, 2)),
        ed_r=dma((FR, 2)),
        rs_s=dma((2,)),
        rs_r=dma((2,)),
        z_s=dma((2,)),
        z_r=dma((2,)),
        ag_s=dma((2,)),
        ag_r=dma((2,)),
    )


def step_kernel(ntm, nsp, names, lists, x_hbm, cot_hbm, w_hbm, c_hbm, mixed_out, fg_out, pg_out, cg_out, *refs):
    r = dict(zip(names, refs))
    nz = nsp // CORES
    npl = ntm * CORES
    part = ROWS // ntm
    chunk = 512 // npl
    frames = FR * ntm
    per = BLOCK // frames
    factor = 1.0 / math.sqrt(frames * ROWS * nsp)

    tm = lax.axis_index("tm")
    sp = lax.axis_index("space")
    z = lax.div(sp, CORES)
    core = lax.rem(sp, CORES)
    left = lax.rem(sp + (nsp - 1), nsp)
    right = lax.rem(sp + 1, nsp)
    place = tm * CORES + core

    def plane_peer(d):
        other = lax.rem(place + d, npl)
        return (lax.div(other, CORES), z * CORES + lax.rem(other, CORES)), other

    def z_peer(d):
        return (tm, lax.rem(z + d, nz) * CORES + core)

    def remote(src, dst, send, recv, device):
        return pltpu.make_async_remote_copy(
            src_ref=src, dst_ref=dst, send_sem=send, recv_sem=recv, device_id=device, device_id_type=MESH
        )

    def loop(count, body):
        def wrapped(i, carry):
            body(i)
            return carry

        lax.fori_loop(0, count, wrapped, 0)

    barrier = pltpu.get_barrier_semaphore()
    pl.semaphore_signal(barrier, inc=1, device_id=(tm, left), device_id_type=MESH)
    pl.semaphore_signal(barrier, inc=1, device_id=(tm, right), device_id_type=MESH)
    loop(npl - 1, lambda i: pl.semaphore_signal(barrier, inc=1, device_id=plane_peer(i + 1)[0], device_id_type=MESH))
    loop(nz - 1, lambda i: pl.semaphore_signal(barrier, inc=1, device_id=z_peer(i + 1), device_id_type=MESH))

    ld = r["ld_sem"]
    own = pl.ds(pl.multiple_of(tm * part, part), part)
    loads = [
        pltpu.make_async_copy(w_hbm.at[0], r["wv"].at[0], ld.at[0]),
        pltpu.make_async_copy(x_hbm, r["xe"].at[1], ld.at[1]),
        pltpu.make_async_copy(c_hbm, r["cv"], ld.at[2]),
        pltpu.make_async_copy(w_hbm.at[1], r["wv"].at[1], ld.at[3]),
        pltpu.make_async_copy(cot_hbm.at[:, own, :], r["hcot"].at[0], ld.at[4]),
    ]
    for item in loads:
        item.start()

    lane_head = lax.broadcasted_iota(jnp.int32, (BLOCK, D), 1) // HD
    for h in range(HEADS):
        r["hm"][h] = jnp.where(lane_head == h, 1.0, 0.0).astype(BF16)
    key_pos = lax.broadcasted_iota(jnp.int32, (BLOCK, 2 * BLOCK), 0) % per
    query_pos = lax.broadcasted_iota(jnp.int32, (BLOCK, 2 * BLOCK), 1) % per
    r["tb"][...] = jnp.where(key_pos == query_pos, 0.0, NEG)

    loads[0].wait()
    r["wt"][0] = r["wv"][0, :, D:].astype(F32).T.astype(BF16)

    pl.semaphore_wait(barrier, 2 + (npl - 1) + (nz - 1))

    halos = [
        remote(x_hbm, r["xe"].at[2], r["halo_s"].at[0], r["halo_r"].at[0], (tm, left)),
        remote(x_hbm, r["xe"].at[0], r["halo_s"].at[1], r["halo_r"].at[1], (tm, right)),
    ]
    for item in halos:
        item.start()

    def cot_copy(d):
        to = lax.rem(tm + d, ntm)
        rows = pl.ds(pl.multiple_of(to * part, part), part)
        return remote(
            cot_hbm.at[:, rows, :], r["hcot"].at[d], r["cot_s"].at[d - 1], r["cot_r"].at[d - 1], (to, sp)
        )

    loop(ntm - 1, lambda i: cot_copy(i + 1).start())

    def project(slot, f):
        normed, inverse = norm(r["xe"][slot, f].astype(F32))
        rows = slice(slot * ROWS, (slot + 1) * ROWS)
        act = normed.astype(BF16)
        r["act"][slot, f] = act
        if slot == 1:
            r["nrm"][f] = normed
            r["rinv"][f] = inverse
            r["q"][f] = nn(act, r["wv"][0, :, 0:D]).astype(BF16)
        r["kv"][f, rows, :] = nn(act, r["wv"][0, :, D:]).astype(BF16)
        r["kvt"][f, :, rows] = nt(r["wt"][0], act).astype(BF16)

    loads[1].wait()
    for f in range(FR):
        project(1, f)
    for f in range(FR):
        for j in range(2):
            for h in range(HEADS):
                r["qs"][2 * f + j, h * BLOCK : (h + 1) * BLOCK, :] = (
                    r["q"][f, j * BLOCK : (j + 1) * BLOCK, :] * r["hm"][h]
                )
    halos[0].wait_recv()
    for f in range(FR):
        project(2, f)
    halos[1].wait_recv()
    for f in range(FR):
        project(0, f)

    def key_rows(j):
        return pl.ds(pl.multiple_of(j * BLOCK, BLOCK), KEYS)

    def biases(f, j):
        out = []
        first = sp * 2 + j - 2
        for e in range(SPAN):
            count = jnp.int32(0)
            for k in range(4):
                count = count + jnp.where(lists[f, j, k] == first + e, 1, 0)
            out.append(
                jnp.where(
                    count == 0,
                    NEG,
                    jnp.where(count == 1, 0.0, jnp.where(count == 2, 1.0, jnp.where(count == 3, math.log2(3.0), 2.0))),
                ).astype(F32)
            )
        return out

    def forward_block(f, j):
        i = 2 * f + j
        rows = key_rows(j)
        bias = biases(f, j)
        outs = []
        for pair in range(HEADS // 2):
            cols = slice(pair * 2 * BLOCK, (pair + 1) * 2 * BLOCK)
            s = r["s"].at[pair % 2]
            s[...] = nt(r["kv"][f, rows, 0:D], r["qs"][i, cols, :])
            top = None
            for e in range(SPAN):
                here = jnp.max(s[e * BLOCK : (e + 1) * BLOCK, :], axis=0, keepdims=True) * SCALE2 + bias[e]
                top = here if top is None else jnp.maximum(top, here)
            total = jnp.zeros((1, 2 * BLOCK), F32)
            for e in range(SPAN):
                block = slice(e * BLOCK, (e + 1) * BLOCK)
                grown = jnp.exp2(s[block, :] * SCALE2 + (bias[e] - top))
                s[block, :] = grown
                total = total + jnp.sum(grown, axis=0, keepdims=True)
            share = 1.0 / total
            for e in range(SPAN):
                block = slice(e * BLOCK, (e + 1) * BLOCK)
                r["probs"][i, block, cols] = (s[block, :] * share).astype(BF16)
            values = r["kvt"][f, D + pair * 2 * HD : D + (pair + 1) * 2 * HD, rows]
            outs.append(diag(nn(values, r["probs"][i, :, cols])))
        out = jnp.concatenate(outs, axis=0)
        r["ot"][i] = out
        r["otb"][:, pl.ds(pl.multiple_of(i * BLOCK, BLOCK), BLOCK)] = out.astype(BF16)
        r["att"][f, pl.ds(pl.multiple_of(j * BLOCK, BLOCK), BLOCK), :] = out.T.astype(BF16)

    def ms_copy(f, d):
        to = lax.rem(tm + d, ntm)
        rows = pl.ds(pl.multiple_of(to * part, part), part)
        return remote(
            r["ms"].at[f, rows, :], r["hist"].at[d, f], r["ms_s"].at[f, d - 1], r["ms_r"].at[f, d - 1], (to, sp)
        )

    loads[2].wait()

    def forward_frame(f):
        loop(2, lambda j: forward_block(f, j))
        mixed = r["xe"][1, f].astype(F32) + nn(r["att"][f], r["cv"][0])
        r["ms"][f] = mixed.astype(BF16)
        r["hist"][0, f] = r["ms"][f, own, :]
        loop(ntm - 1, lambda i: ms_copy(f, i + 1).start())

    loop(FR, forward_frame)

    for f in range(FR):
        for slot in range(3):
            r["act_t"][f, :, slot * ROWS : (slot + 1) * ROWS] = r["act"][slot, f].astype(F32).T.astype(BF16)
    loads[3].wait()
    r["wt"][1] = r["wv"][1, :, D:].astype(F32).T.astype(BF16)
    loads[4].wait()
    loop(ntm - 1, lambda i: cot_copy(i + 1).wait_recv())

    def regroup(src, dst):
        for d in range(ntm):
            for f in range(FR):
                frame = d * FR + f
                rows = src[d, f].astype(F32)
                for g in range(GROUPS):
                    dst[g, frame * per : (frame + 1) * per, :] = rows[g * per : (g + 1) * per]

    def ungroup(src, dst):
        for d in range(ntm):
            for f in range(FR):
                frame = d * FR + f
                dst[d, f] = jnp.concatenate(
                    [src[g, frame * per : (frame + 1) * per, :] for g in range(GROUPS)], axis=0
                ).astype(BF16)

    regroup(r["hcot"], r["ct"])
    for g in range(GROUPS):
        rows = slice(g * BLOCK, (g + 1) * BLOCK)
        cot = r["ct"][g].astype(BF16)
        r["tdo"][rows, :] = nt(cot, r["cv"][1]).astype(BF16)
        r["tdot"][:, rows] = nt(r["cv"][1], cot).astype(BF16)

    for f in range(FR):
        loop(ntm - 1, lambda i, f=f: ms_copy(f, i + 1).wait_recv())
    regroup(r["hist"], r["xt"])
    for g in range(GROUPS):
        rows = slice(g * BLOCK, (g + 1) * BLOCK)
        normed, inverse = norm(r["xt"][g])
        r["tnrm"][rows, :] = normed
        r["trinv"][rows, :] = inverse
        r["tact"][rows, :] = normed.astype(BF16)
    r["tp"][...] = nn(r["tact"][...], r["wv"][1]).astype(BF16)
    r["tkvt"][...] = nt(r["wt"][1], r["tact"][...]).astype(BF16)

    def time_group(g):
        rows = pl.ds(pl.multiple_of(g * BLOCK, BLOCK), BLOCK)
        query = r["tp"][rows, 0:D]
        keys = r["tp"][rows, D : 2 * D]
        values = r["tp"][rows, 2 * D : 3 * D]
        grad = r["tdo"][rows, :]
        for h in range(HEADS):
            r["tqs"][h * BLOCK : (h + 1) * BLOCK, :] = query * r["hm"][h]
            r["dos"][h * BLOCK : (h + 1) * BLOCK, :] = grad * r["hm"][h]
        outs = []
        parts = []
        for pair in range(HEADS // 2):
            cols = slice(pair * 2 * BLOCK, (pair + 1) * 2 * BLOCK)
            scores = nt(keys, r["tqs"][cols, :]) * SCALE2 + r["tb"][...]
            grown = jnp.exp2(scores - jnp.max(scores, axis=0, keepdims=True))
            share = 1.0 / jnp.sum(grown, axis=0, keepdims=True)
            probs = (grown * share).astype(BF16)
            parts.append(probs)
            outs.append(diag(nn(r["tkvt"][D + pair * 2 * HD : D + (pair + 1) * 2 * HD, rows], probs)))
        out = jnp.concatenate(outs, axis=0)
        r["tot"][:, rows] = out.astype(BF16)
        r["tatt"][rows, :] = out.T.astype(BF16)
        delta = head_sums(out * r["tdot"][:, rows].astype(F32))
        query_grads = []
        key_grad = None
        value_grad = None
        for pair in range(HEADS // 2):
            cols = slice(pair * 2 * BLOCK, (pair + 1) * 2 * BLOCK)
            dprob = nt(values, r["dos"][cols, :])
            shift = jnp.concatenate([delta[2 * pair : 2 * pair + 1], delta[2 * pair + 1 : 2 * pair + 2]], axis=1)
            dscore = (parts[pair].astype(F32) * (dprob - shift)).astype(BF16)
            query_grads.append(diag(nn(r["tkvt"][pair * 2 * HD : (pair + 1) * 2 * HD, rows], dscore)))
            more_key = nn(dscore, r["tqs"][cols, :])
            more_value = nn(parts[pair], r["dos"][cols, :])
            key_grad = more_key if key_grad is None else key_grad + more_key
            value_grad = more_value if value_grad is None else value_grad + more_value
        query_grad = jnp.concatenate(query_grads, axis=0).T
        r["tdp"][rows, 0:D] = (query_grad * SCALE).astype(BF16)
        r["tdp"][rows, D : 2 * D] = (key_grad * SCALE).astype(BF16)
        r["tdp"][rows, 2 * D : 3 * D] = value_grad.astype(BF16)

    loop(GROUPS, time_group)

    def back_rows(base, d):
        return base.at[:, own, :]

    def mg_copy(d):
        return remote(
            r["mgs"].at[d], r["mg"].at[:, own, :], r["mg_s"].at[d - 1], r["mg_r"].at[d - 1],
            (lax.rem(tm + (ntm - d), ntm), sp),
        )

    def mf_copy(d):
        return remote(
            r["mfs"].at[d], mixed_out.at[:, own, :], r["mf_s"].at[d - 1], r["mf_r"].at[d - 1],
            (lax.rem(tm + (ntm - d), ntm), sp),
        )

    for g in range(GROUPS):
        rows = slice(g * BLOCK, (g + 1) * BLOCK)
        act_grad = nt(r["tdp"][rows, :], r["wv"][1])
        r["tmix"][g] = r["ct"][g] + norm_back(act_grad, r["tnrm"][rows, :], r["trinv"][rows, :])
    ungroup(r["tmix"], r["mgs"])
    loop(ntm - 1, lambda i: mg_copy(i + 1).start())
    r["mg"][:, own, :] = r["mgs"][0]

    for g in range(GROUPS):
        rows = slice(g * BLOCK, (g + 1) * BLOCK)
        r["tmix"][g] = r["xt"][g] + nn(r["tatt"][rows, :], r["cv"][1])
    ungroup(r["tmix"], r["mfs"])
    loop(ntm - 1, lambda i: mf_copy(i + 1).start())
    keep = pltpu.make_async_copy(r["mfs"].at[0], mixed_out.at[:, own, :], ld.at[5])
    keep.start()

    turned = r["tact"][...].astype(F32).T.astype(BF16)
    r["g"][0, 0:D, :] = nn(turned, r["tdp"][:, D:]).astype(BF16)
    r["g"][0, D:, 0:D] = nn(turned, r["tdp"][:, 0:D]).astype(BF16)
    cots = r["ct"][...].reshape(GROUPS * BLOCK, D).astype(BF16)
    r["g"][0, D:, D:] = nn(r["tot"][...], cots).astype(BF16)

    my_chunk = pl.ds(pl.multiple_of(place * chunk, chunk), chunk)

    def rs_copy(a, d):
        device, other = plane_peer(d)
        rows = pl.ds(pl.multiple_of(other * chunk, chunk), chunk)
        return remote(r["g"].at[a, rows, :], r["rs"].at[a, d - 1], r["rs_s"].at[a], r["rs_r"].at[a], device)

    def z_copy(a, d):
        return remote(r["zb"].at[a, z], r["zb"].at[a, z], r["z_s"].at[a], r["z_r"].at[a], z_peer(d))

    def ag_copy(a, d):
        device, _ = plane_peer(d)
        return remote(r["fin"].at[a, my_chunk, :], r["fin"].at[a, my_chunk, :], r["ag_s"].at[a], r["ag_r"].at[a], device)

    def drain(ref, sem):
        pltpu.make_async_copy(ref, ref, sem).wait()

    def reduce_start(a):
        loop(npl - 1, lambda i: rs_copy(a, i + 1).start())

    def reduce_middle(a):
        drain(r["rs"].at[a], r["rs_r"].at[a])
        total = r["g"][a, my_chunk, :].astype(F32)
        for d in range(npl - 1):
            total = total + r["rs"][a, d].astype(F32)
        r["zb"][a, z] = total.astype(BF16)
        loop(nz - 1, lambda i: z_copy(a, i + 1).start())

    def reduce_share(a):
        drain(r["zb"].at[a, 0 : nz - 1], r["z_r"].at[a])
        total = r["zb"][a, 0].astype(F32)
        for k in range(1, nz):
            total = total + r["zb"][a, k].astype(F32)
        r["fin"][a, my_chunk, :] = total.astype(BF16)
        loop(npl - 1, lambda i: ag_copy(a, i + 1).start())

    def reduce_end(a, layer):
        drain(r["fin"].at[a, 0 : (npl - 1) * chunk, :], r["ag_r"].at[a])
        pg_out[layer, :, D:] = r["fin"][a, 0:D, :].astype(F32) * factor
        pg_out[layer, :, 0:D] = r["fin"][a, D:, 0:D].astype(F32) * factor
        cg_out[layer] = r["fin"][a, D:, D:].astype(F32) * factor

    def reduce_drain(a):
        drain(r["rs"].at[a], r["rs_s"].at[a])
        drain(r["zb"].at[a, 0 : nz - 1], r["z_s"].at[a])
        drain(r["fin"].at[a, 0 : (npl - 1) * chunk, :], r["ag_s"].at[a])

    reduce_start(0)

    r["dkv"][...] = jnp.zeros_like(r["dkv"])

    def mg_arrival(d):
        rows = pl.ds(pl.multiple_of(lax.rem(tm + d, ntm) * part, part), part)
        return remote(r["mgs"].at[d], r["mg"].at[:, rows, :], r["mg_s"].at[d - 1], r["mg_r"].at[d - 1], (tm, sp))

    loop(ntm - 1, lambda i: mg_arrival(i + 1).wait_recv())

    for f in range(FR):
        grad = r["mg"][f]
        r["do"][f] = nt(grad, r["cv"][0]).astype(BF16)
        r["dot_t"][:, f * ROWS : (f + 1) * ROWS] = nt(r["cv"][0], grad).astype(BF16)

    def backward_block(f, j):
        i = 2 * f + j
        rows = key_rows(j)
        mine = pl.ds(pl.multiple_of(j * BLOCK, BLOCK), BLOCK)
        grad = r["do"][f, mine, :]
        for h in range(HEADS):
            r["dos"][h * BLOCK : (h + 1) * BLOCK, :] = grad * r["hm"][h]
        lanes = pl.ds(pl.multiple_of(i * BLOCK, BLOCK), BLOCK)
        delta = head_sums(r["ot"][i] * r["dot_t"][:, lanes].astype(F32))
        outs = []
        for pair in range(HEADS // 2):
            cols = slice(pair * 2 * BLOCK, (pair + 1) * 2 * BLOCK)
            s = r["s"].at[pair % 2]
            s[...] = nt(r["kv"][f, rows, D:], r["dos"][cols, :])
            shift = jnp.concatenate([delta[2 * pair : 2 * pair + 1], delta[2 * pair + 1 : 2 * pair + 2]], axis=1)
            for e in range(SPAN):
                block = slice(e * BLOCK, (e + 1) * BLOCK)
                r["ds"][block, cols] = (r["probs"][i, block, cols].astype(F32) * (s[block, :] - shift)).astype(BF16)
            outs.append(diag(nn(r["kvt"][f, pair * 2 * HD : (pair + 1) * 2 * HD, rows], r["ds"][:, cols])))
        r["dq"][f, mine, :] = (jnp.concatenate(outs, axis=0) * SCALE).T.astype(BF16)
        r["dkv"][f, rows, 0:D] += nn(r["ds"][...], r["qs"][i]) * SCALE
        r["dkv"][f, rows, D:] += nn(r["probs"][i], r["dos"][...])

    def edge_copies(f):
        return [
            remote(r["dkvb"].at[f, 0:ROWS, :], r["er"].at[f, 1], r["ed_s"].at[f, 0], r["ed_r"].at[f, 0], (tm, left)),
            remote(
                r["dkvb"].at[f, 2 * ROWS :, :], r["er"].at[f, 0], r["ed_s"].at[f, 1], r["ed_r"].at[f, 1], (tm, right)
            ),
        ]

    def backward_frame(f):
        loop(2, lambda j: backward_block(f, j))
        r["dkvb"][f] = r["dkv"][f].astype(BF16)
        for item in edge_copies(f):
            item.start()

    backward_frame(0)
    reduce_middle(0)
    backward_frame(1)
    reduce_share(0)

    inward = nn(r["act_t"][0], r["dkvb"][0]) + nn(r["act_t"][1], r["dkvb"][1])
    r["g"][1, 0:D, :] = inward.astype(BF16)
    inward = nn(r["act_t"][0, :, ROWS : 2 * ROWS], r["dq"][0]) + nn(r["act_t"][1, :, ROWS : 2 * ROWS], r["dq"][1])
    r["g"][1, D:, 0:D] = inward.astype(BF16)
    outward = nn(r["otb"][:, 0:ROWS], r["mg"][0]) + nn(r["otb"][:, ROWS:], r["mg"][1])
    r["g"][1, D:, D:] = outward.astype(BF16)
    reduce_start(1)

    for f in range(FR):
        for item in edge_copies(f):
            item.wait_recv()
        pair_grad = r["dkv"][f, ROWS : 2 * ROWS, :] + r["er"][f, 0].astype(F32) + r["er"][f, 1].astype(F32)
        act_grad = nt(r["dq"][f], r["wv"][0, :, 0:D]) + nt(pair_grad.astype(BF16), r["wv"][0, :, D:])
        fg_out[f] = (r["mg"][f].astype(F32) + norm_back(act_grad, r["nrm"][f], r["rinv"][f])).astype(BF16)

    reduce_middle(1)
    reduce_end(0, 1)
    reduce_share(1)

    keep.wait()

    def mf_arrival(d):
        rows = pl.ds(pl.multiple_of(lax.rem(tm + d, ntm) * part, part), part)
        return remote(r["mfs"].at[d], mixed_out.at[:, rows, :], r["mf_s"].at[d - 1], r["mf_r"].at[d - 1], (tm, sp))

    loop(ntm - 1, lambda i: mf_arrival(i + 1).wait_recv())
    loop(ntm - 1, lambda i: mf_copy(i + 1).wait_send())
    loop(ntm - 1, lambda i: mg_copy(i + 1).wait_send())
    loop(ntm - 1, lambda i: cot_copy(i + 1).wait_send())
    for f in range(FR):
        loop(ntm - 1, lambda i, f=f: ms_copy(f, i + 1).wait_send())
        for item in edge_copies(f):
            item.wait_send()
    for item in halos:
        item.wait_send()
    reduce_drain(0)

    reduce_end(1, 0)
    reduce_drain(1)


def per_device(ntm, nsp, wave_field, cotangent, block_lists, project_weights, combine_weights):
    shapes = scratch_shapes(ntm, nsp)
    names = tuple(shapes)
    anywhere = pl.BlockSpec(memory_space=pl.ANY)
    vmem = pl.BlockSpec(memory_space=pltpu.VMEM)
    return pl.pallas_call(
        functools.partial(step_kernel, ntm, nsp, names),
        out_shape=(
            jax.ShapeDtypeStruct((FR, ROWS, D), BF16),
            jax.ShapeDtypeStruct((FR, ROWS, D), BF16),
            jax.ShapeDtypeStruct((2, D, 3 * D), F32),
            jax.ShapeDtypeStruct((2, D, D), F32),
        ),
        in_specs=[pl.BlockSpec(memory_space=pltpu.SMEM), anywhere, anywhere, anywhere, anywhere],
        out_specs=(anywhere, vmem, vmem, vmem),
        scratch_shapes=list(shapes.values()),
        compiler_params=pltpu.CompilerParams(
            collective_id=0, has_side_effects=True, vmem_limit_bytes=60 * 1024 * 1024
        ),
        name="cuboid_step",
    )(block_lists, wave_field, cotangent, project_weights, combine_weights)


def solution(mesh):
    in_specs = (P("tm", "space", None), P("tm", "space", None), P("tm", "space", None), P(), P())
    out_specs = (P("tm", "space", None), P("tm", "space", None), P(), P())
    return jax.shard_map(
        functools.partial(per_device, mesh.shape["tm"], mesh.shape["space"]),
        mesh=mesh,
        in_specs=in_specs,
        out_specs=out_specs,
        check_vma=False,
    )
```

time: 571 us -> 107 us (0.19); the launches traced: 562 us -> 107 us
  waiting for transfers between devices: 292 us -> 0 us
  Pallas kernels: 0 us -> 99.6 us
  local copies, waits for them, and re-layouts: 81.3 us -> 6.84 us
  other arithmetic: 73.4 us -> 0 us
  matrix products: 70.6 us -> 0 us
  starting transfers between devices: 29.6 us -> 0 us
  between operations: 15.3 us -> 0.64 us
    psum x1 -> x0, waiting for transfers between devices: 268 us -> none  [per_device(): lax.psum((space_inward, space_outward, time_inward, time_outward), ('tm',...]
    pallas_call x0 -> x1, Pallas kernels: none -> 99.6 us  [per_device(): pl.pallas_call(functools.partial(step_kernel, ntm, nsp, names), out_shape...]
    dot_general x26 -> x0, matrix products: 70.6 us -> none  [the longest x12 53.7 us: einsum_wide(): jnp.einsum(formula, left_op, right_op, preferred_element_type=jnp.float32)]
    scatter-add x1 -> x0, other arithmetic: 38.2 us -> none  [backward_group(): return (running.at[group_rows].add(key_tiles), grad_query)]
    reshape x8 -> x0, local copies, waits for them, and re-layouts: 32.9 us -> none  [the longest x1 16.9 us: backward_group(): jnp.stack([grad_keys, grad_values], axis=2)]
    all_to_all x4 -> x0, waiting for transfers between devices: 23.7 us -> none  [the longest x1 9.79 us: per_device(): lax.all_to_all(cotangent, 'tm', split_axis=1, concat_axis=0, tiled=True)]
    all_to_all x4 -> x0, starting transfers between devices: 17.1 us -> none  [the longest x1 6 us: per_device(): lax.all_to_all(cotangent, 'tm', split_axis=1, concat_axis=0, tiled=True)]
    another operation x2 -> x0, local copies, waits for them, and re-layouts: 13.4 us -> none  [the longest x1 12.6 us: backward_group(): jnp.stack([grad_keys, grad_values], axis=2)]
  transfers between devices with their start and end apart: 9 -> 0, of which waited for: 4 -> 0; matrix products, arithmetic and copies ran while one was open for 22% -> 0% of each run, Pallas kernels for 0% -> 0%
where the time goes in v1:
time: 107 us
  Pallas kernels  99.6 us (93%)
  local copies, waits for them, and re-layouts  6.84 us (6%)
    pallas_call x1, Pallas kernels, per_device(): pl.pallas_call(functools.partial(step_kernel, ntm, nsp, names), out_shape...  99.6 us
    unnamed x6, local copies, waits for them, and re-layouts  6.84 us

profile of v1, /device:TPU:1, one launch (start us, length us, event | category | flops | bytes accessed | tf_op | source)
XLA Modules:
  0.0 107.1 jit_solution(2946987300199124810)
XLA Ops:
  0.6 99.6 %cuboid_step.1 = (bf16[2,256,256]{2,1,0:T(8,128)(2,1)}, bf16[2,256,256]{2,1,0:T(8,128)(2,1)}, f32[2,256,768]{2,1,0:T(8,128)}, f32[2,256,256]{2,1,0:T(8,128)}) custom-call(s32[2,2,4]{2,1,0:T(2,128)} %lists.1, bf16[2,256,256]{2,1,0:T(8,128)(2,1)} %x_hbm.1, bf16[2,256,256]{2,1,0:T(8,128)(2,1)} %cot_hbm.1, bf16[2,256,768]{2,1,0:T(8,128)(2,1)} %w_hbm.1, ...), custom_call_target="tpu_custom_call" | custom-call | tf_op jit(solution)/shard_map/cuboid_step/pallas_call | solution.py:591
  100.3 1.7 %copy.13 = bf16[2,256,256]{2,1,0:T(8,128)(2,1)} copy(bf16[2,256,256]{2,1,0:T(8,128)(2,1)} %get-tuple-element.8) | data formatting | bytes 524288
  101.9 1.7 %copy.14 = bf16[2,256,256]{2,1,0:T(8,128)(2,1)} copy(bf16[2,256,256]{2,1,0:T(8,128)(2,1)} %get-tuple-element.9) | data formatting | bytes 524288
  103.6 0.0 copy-start
  103.6 2.7 %copy.15 = f32[2,256,768]{2,1,0:T(8,128)} copy(f32[2,256,768]{2,1,0:T(8,128)} %get-tuple-element.10) | data formatting | bytes 3145728
  106.3 0.0 copy-done
  106.3 0.8 copy.16
Async XLA Ops:
  103.6 2.7 %copy-start = (f32[2,256,256]{2,1,0:T(8,128)S(1)}, f32[2,256,256]{2,1,0:T(8,128)}, u32[]{:S(2)}) copy-start(f32[2,256,256]{2,1,0:T(8,128)} %get-tuple-element.11) | copy-start | bytes 1572868

commit v2 on v1

--- a/solution.py
+++ b/solution.py
@@ -58,9 +58,9 @@
 
 def scratch_shapes(ntm, nsp):
     nz = nsp // CORES
-    npl = ntm * CORES
+    npl = ntm * 2
     part = ROWS // ntm
-    chunk = 512 // npl
+    chunk = 256 // npl
     dma = pltpu.SemaphoreType.DMA
     vm = pltpu.VMEM
     return dict(
@@ -77,7 +77,9 @@
         kv=vm((FR, 3 * ROWS, 2 * D), BF16),
         kvt=vm((FR, 2 * D, 3 * ROWS), BF16),
         qs=vm((4, HEADS * BLOCK, D), BF16),
-        dos=vm((HEADS * BLOCK, D), BF16),
+        dos=vm((4, HEADS * BLOCK, D), BF16),
+        share=vm((4, HEADS, BLOCK), F32),
+        delta=vm((4, HEADS, BLOCK), F32),
         probs=vm((4, KEYS, HEADS * BLOCK), BF16),
         ds=vm((KEYS, HEADS * BLOCK), BF16),
         s=vm((2, KEYS, 2 * BLOCK), F32),
@@ -100,18 +102,22 @@
         tot=vm((D, GROUPS * BLOCK), BF16),
         tatt=vm((GROUPS * BLOCK, D), BF16),
         tdp=vm((GROUPS * BLOCK, 3 * D), BF16),
-        tqs=vm((HEADS * BLOCK, D), BF16),
+        tqs=vm((GROUPS, HEADS * BLOCK, D), BF16),
+        tdos=vm((GROUPS, HEADS * BLOCK, D), BF16),
+        tprobs=vm((GROUPS, BLOCK, HEADS * BLOCK), BF16),
+        tds=vm((GROUPS, BLOCK, HEADS * BLOCK), BF16),
         tmix=vm((GROUPS, BLOCK, D), F32),
         mfs=vm((ntm, FR, part, D), BF16),
         mgs=vm((ntm, FR, part, D), BF16),
         mg=vm((FR, ROWS, D), BF16),
-        do=vm((FR, ROWS, D), BF16),
-        dot_t=vm((D, FR * ROWS), BF16),
         dq=vm((FR, ROWS, D), BF16),
         dkv=vm((FR, 3 * ROWS, 2 * D), F32),
         dkvb=vm((FR, 3 * ROWS, 2 * D), BF16),
         er=vm((FR, 2, ROWS, 2 * D), BF16),
         g=vm((2, 512, 512), BF16),
+        pr=vm((2, 256, 512), BF16),
+        h=vm((2, 256, 512), BF16),
+        fg=vm((FR, ROWS, D), BF16),
         rs=vm((2, npl - 1, chunk, 512), BF16),
         zb=vm((2, nz, chunk, 512), BF16),
         fin=vm((2, 512, 512), BF16),
@@ -128,6 +134,11 @@
         mg_r=dma((ntm - 1,)),
         ed_s=dma((FR, 2)),
         ed_r=dma((FR, 2)),
+        pr_s=dma((2,)),
+        pr_r=dma((2,)),
+        pg_s=dma((2,)),
+        pg_r=dma((2,)),
+        out_s=dma((4,)),
         rs_s=dma((2,)),
         rs_r=dma((2,)),
         z_s=dma((2,)),
@@ -137,30 +148,31 @@
     )
 
 
-def step_kernel(ntm, nsp, names, lists, x_hbm, cot_hbm, w_hbm, c_hbm, mixed_out, fg_out, pg_out, cg_out, *refs):
+def step_kernel(ntm, nsp, names, lists, x_hbm, cot_hbm, w_hbm, c_hbm, mixed_out, fg_out, fin_out, *refs):
     r = dict(zip(names, refs))
     nz = nsp // CORES
-    npl = ntm * CORES
+    npl = ntm * 2
     part = ROWS // ntm
-    chunk = 512 // npl
+    chunk = 256 // npl
     frames = FR * ntm
     per = BLOCK // frames
-    factor = 1.0 / math.sqrt(frames * ROWS * nsp)
 
     tm = lax.axis_index("tm")
     sp = lax.axis_index("space")
     z = lax.div(sp, CORES)
-    core = lax.rem(sp, CORES)
+    quarter = lax.rem(sp, CORES)
+    core = lax.rem(sp, 2)
+    partner = sp + 1 - 2 * core
     left = lax.rem(sp + (nsp - 1), nsp)
     right = lax.rem(sp + 1, nsp)
-    place = tm * CORES + core
+    place = tm * 2 + lax.div(quarter, 2)
 
     def plane_peer(d):
         other = lax.rem(place + d, npl)
-        return (lax.div(other, CORES), z * CORES + lax.rem(other, CORES)), other
+        return (lax.div(other, 2), z * CORES + lax.rem(other, 2) * 2 + core), other
 
     def z_peer(d):
-        return (tm, lax.rem(z + d, nz) * CORES + core)
+        return (tm, lax.rem(z + d, nz) * CORES + quarter)
 
     def remote(src, dst, send, recv, device):
         return pltpu.make_async_remote_copy(
@@ -218,8 +230,6 @@
             cot_hbm.at[:, rows, :], r["hcot"].at[d], r["cot_s"].at[d - 1], r["cot_r"].at[d - 1], (to, sp)
         )
 
-    loop(ntm - 1, lambda i: cot_copy(i + 1).start())
-
     def project(slot, f):
         normed, inverse = norm(r["xe"][slot, f].astype(F32))
         rows = slice(slot * ROWS, (slot + 1) * ROWS)
@@ -245,6 +255,7 @@
     for f in range(FR):
         project(2, f)
     halos[1].wait_recv()
+    loop(ntm - 1, lambda i: cot_copy(i + 1).start())
     for f in range(FR):
         project(0, f)
 
@@ -275,23 +286,23 @@
         for pair in range(HEADS // 2):
             cols = slice(pair * 2 * BLOCK, (pair + 1) * 2 * BLOCK)
             s = r["s"].at[pair % 2]
-            s[...] = nt(r["kv"][f, rows, 0:D], r["qs"][i, cols, :])
+            scores = nt(r["kv"][f, rows, 0:D], r["qs"][i, cols, :])
+            s[...] = scores
             top = None
             for e in range(SPAN):
-                here = jnp.max(s[e * BLOCK : (e + 1) * BLOCK, :], axis=0, keepdims=True) * SCALE2 + bias[e]
+                here = jnp.max(scores[e * BLOCK : (e + 1) * BLOCK, :], axis=0, keepdims=True) * SCALE2 + bias[e]
                 top = here if top is None else jnp.maximum(top, here)
             total = jnp.zeros((1, 2 * BLOCK), F32)
             for e in range(SPAN):
                 block = slice(e * BLOCK, (e + 1) * BLOCK)
                 grown = jnp.exp2(s[block, :] * SCALE2 + (bias[e] - top))
-                s[block, :] = grown
+                r["probs"][i, block, cols] = grown.astype(BF16)
                 total = total + jnp.sum(grown, axis=0, keepdims=True)
             share = 1.0 / total
-            for e in range(SPAN):
-                block = slice(e * BLOCK, (e + 1) * BLOCK)
-                r["probs"][i, block, cols] = (s[block, :] * share).astype(BF16)
+            r["share"][i, 2 * pair : 2 * pair + 1, :] = share[:, 0:BLOCK]
+            r["share"][i, 2 * pair + 1 : 2 * pair + 2, :] = share[:, BLOCK:]
             values = r["kvt"][f, D + pair * 2 * HD : D + (pair + 1) * 2 * HD, rows]
-            outs.append(diag(nn(values, r["probs"][i, :, cols])))
+            outs.append(diag(nn(values, r["probs"][i, :, cols]) * share))
         out = jnp.concatenate(outs, axis=0)
         r["ot"][i] = out
         r["otb"][:, pl.ds(pl.multiple_of(i * BLOCK, BLOCK), BLOCK)] = out.astype(BF16)
@@ -343,66 +354,73 @@
     for g in range(GROUPS):
         rows = slice(g * BLOCK, (g + 1) * BLOCK)
         cot = r["ct"][g].astype(BF16)
-        r["tdo"][rows, :] = nt(cot, r["cv"][1]).astype(BF16)
+        grad = nt(cot, r["cv"][1]).astype(BF16)
+        for h in range(HEADS):
+            r["tdos"][g, h * BLOCK : (h + 1) * BLOCK, :] = grad * r["hm"][h]
         r["tdot"][:, rows] = nt(r["cv"][1], cot).astype(BF16)
 
     for f in range(FR):
         loop(ntm - 1, lambda i, f=f: ms_copy(f, i + 1).wait_recv())
-    regroup(r["hist"], r["xt"])
-    for g in range(GROUPS):
-        rows = slice(g * BLOCK, (g + 1) * BLOCK)
-        normed, inverse = norm(r["xt"][g])
-        r["tnrm"][rows, :] = normed
-        r["trinv"][rows, :] = inverse
-        r["tact"][rows, :] = normed.astype(BF16)
+        for d in range(ntm):
+            frame = d * FR + f
+            block = r["hist"][d, f].astype(F32)
+            normed, inverse = norm(block)
+            for g in range(GROUPS):
+                to = slice(frame * per, (frame + 1) * per)
+                at = slice(g * BLOCK + frame * per, g * BLOCK + (frame + 1) * per)
+                mine = slice(g * per, (g + 1) * per)
+                r["xt"][g, to, :] = block[mine]
+                r["tnrm"][at, :] = normed[mine]
+                r["trinv"][at, :] = inverse[mine]
+    r["tact"][...] = r["tnrm"][...].astype(BF16)
     r["tp"][...] = nn(r["tact"][...], r["wv"][1]).astype(BF16)
     r["tkvt"][...] = nt(r["wt"][1], r["tact"][...]).astype(BF16)
 
-    def time_group(g):
-        rows = pl.ds(pl.multiple_of(g * BLOCK, BLOCK), BLOCK)
+    def time_scores(g):
+        rows = slice(g * BLOCK, (g + 1) * BLOCK)
         query = r["tp"][rows, 0:D]
-        keys = r["tp"][rows, D : 2 * D]
-        values = r["tp"][rows, 2 * D : 3 * D]
-        grad = r["tdo"][rows, :]
         for h in range(HEADS):
-            r["tqs"][h * BLOCK : (h + 1) * BLOCK, :] = query * r["hm"][h]
-            r["dos"][h * BLOCK : (h + 1) * BLOCK, :] = grad * r["hm"][h]
-        outs = []
-        parts = []
+            r["tqs"][g, h * BLOCK : (h + 1) * BLOCK, :] = query * r["hm"][h]
         for pair in range(HEADS // 2):
             cols = slice(pair * 2 * BLOCK, (pair + 1) * 2 * BLOCK)
-            scores = nt(keys, r["tqs"][cols, :]) * SCALE2 + r["tb"][...]
+            scores = nt(r["tp"][rows, D : 2 * D], r["tqs"][g, cols, :]) * SCALE2 + r["tb"][...]
             grown = jnp.exp2(scores - jnp.max(scores, axis=0, keepdims=True))
             share = 1.0 / jnp.sum(grown, axis=0, keepdims=True)
-            probs = (grown * share).astype(BF16)
-            parts.append(probs)
-            outs.append(diag(nn(r["tkvt"][D + pair * 2 * HD : D + (pair + 1) * 2 * HD, rows], probs)))
+            r["tprobs"][g, :, cols] = (grown * share).astype(BF16)
+
+    def time_out(g):
+        rows = slice(g * BLOCK, (g + 1) * BLOCK)
+        outs = []
+        for pair in range(HEADS // 2):
+            cols = slice(pair * 2 * BLOCK, (pair + 1) * 2 * BLOCK)
+            values = r["tkvt"][D + pair * 2 * HD : D + (pair + 1) * 2 * HD, rows]
+            outs.append(diag(nn(values, r["tprobs"][g, :, cols])))
         out = jnp.concatenate(outs, axis=0)
         r["tot"][:, rows] = out.astype(BF16)
         r["tatt"][rows, :] = out.T.astype(BF16)
         delta = head_sums(out * r["tdot"][:, rows].astype(F32))
-        query_grads = []
-        key_grad = None
-        value_grad = None
         for pair in range(HEADS // 2):
             cols = slice(pair * 2 * BLOCK, (pair + 1) * 2 * BLOCK)
-            dprob = nt(values, r["dos"][cols, :])
+            dprob = nt(r["tp"][rows, 2 * D :], r["tdos"][g, cols, :])
             shift = jnp.concatenate([delta[2 * pair : 2 * pair + 1], delta[2 * pair + 1 : 2 * pair + 2]], axis=1)
-            dscore = (parts[pair].astype(F32) * (dprob - shift)).astype(BF16)
-            query_grads.append(diag(nn(r["tkvt"][pair * 2 * HD : (pair + 1) * 2 * HD, rows], dscore)))
-            more_key = nn(dscore, r["tqs"][cols, :])
-            more_value = nn(parts[pair], r["dos"][cols, :])
-            key_grad = more_key if key_grad is None else key_grad + more_key
-            value_grad = more_value if value_grad is None else value_grad + more_value
-        query_grad = jnp.concatenate(query_grads, axis=0).T
-        r["tdp"][rows, 0:D] = (query_grad * SCALE).astype(BF16)
-        r["tdp"][rows, D : 2 * D] = (key_grad * SCALE).astype(BF16)
-        r["tdp"][rows, 2 * D : 3 * D] = value_grad.astype(BF16)
-
-    loop(GROUPS, time_group)
-
-    def back_rows(base, d):
-        return base.at[:, own, :]
+            r["tds"][g, :, cols] = (r["tprobs"][g, :, cols].astype(F32) * (dprob - shift)).astype(BF16)
+
+    def time_grads(g):
+        rows = slice(g * BLOCK, (g + 1) * BLOCK)
+        outs = []
+        for pair in range(HEADS // 2):
+            cols = slice(pair * 2 * BLOCK, (pair + 1) * 2 * BLOCK)
+            outs.append(diag(nn(r["tkvt"][pair * 2 * HD : (pair + 1) * 2 * HD, rows], r["tds"][g, :, cols])))
+        r["tdp"][rows, 0:D] = (jnp.concatenate(outs, axis=0) * SCALE).T.astype(BF16)
+        r["tdp"][rows, D : 2 * D] = (nn(r["tds"][g], r["tqs"][g]) * SCALE).astype(BF16)
+        r["tdp"][rows, 2 * D : 3 * D] = nn(r["tprobs"][g], r["tdos"][g]).astype(BF16)
+
+    for g in range(GROUPS):
+        time_scores(g)
+    for g in range(GROUPS):
+        time_out(g)
+    for g in range(GROUPS):
+        time_grads(g)
 
     def mg_copy(d):
         return remote(
@@ -428,7 +446,6 @@
         rows = slice(g * BLOCK, (g + 1) * BLOCK)
         r["tmix"][g] = r["xt"][g] + nn(r["tatt"][rows, :], r["cv"][1])
     ungroup(r["tmix"], r["mfs"])
-    loop(ntm - 1, lambda i: mf_copy(i + 1).start())
     keep = pltpu.make_async_copy(r["mfs"].at[0], mixed_out.at[:, own, :], ld.at[5])
     keep.start()
 
@@ -438,12 +455,18 @@
     cots = r["ct"][...].reshape(GROUPS * BLOCK, D).astype(BF16)
     r["g"][0, D:, D:] = nn(r["tot"][...], cots).astype(BF16)
 
-    my_chunk = pl.ds(pl.multiple_of(place * chunk, chunk), chunk)
+    my_half = pl.ds(pl.multiple_of(core * 256, 256), 256)
+    other_half = pl.ds(pl.multiple_of((1 - core) * 256, 256), 256)
+    in_half = pl.ds(pl.multiple_of(place * chunk, chunk), chunk)
+    my_chunk = pl.ds(pl.multiple_of(core * 256 + place * chunk, chunk), chunk)
+
+    def pair_copy(a):
+        return remote(r["g"].at[a, other_half, :], r["pr"].at[a], r["pr_s"].at[a], r["pr_r"].at[a], (tm, partner))
 
     def rs_copy(a, d):
         device, other = plane_peer(d)
         rows = pl.ds(pl.multiple_of(other * chunk, chunk), chunk)
-        return remote(r["g"].at[a, rows, :], r["rs"].at[a, d - 1], r["rs_s"].at[a], r["rs_r"].at[a], device)
+        return remote(r["h"].at[a, rows, :], r["rs"].at[a, d - 1], r["rs_s"].at[a], r["rs_r"].at[a], device)
 
     def z_copy(a, d):
         return remote(r["zb"].at[a, z], r["zb"].at[a, z], r["z_s"].at[a], r["z_r"].at[a], z_peer(d))
@@ -452,15 +475,22 @@
         device, _ = plane_peer(d)
         return remote(r["fin"].at[a, my_chunk, :], r["fin"].at[a, my_chunk, :], r["ag_s"].at[a], r["ag_r"].at[a], device)
 
+    def join_copy(a):
+        return remote(
+            r["fin"].at[a, my_half, :], r["fin"].at[a, my_half, :], r["pg_s"].at[a], r["pg_r"].at[a], (tm, partner)
+        )
+
     def drain(ref, sem):
         pltpu.make_async_copy(ref, ref, sem).wait()
 
-    def reduce_start(a):
+    def reduce_pair(a):
+        pair_copy(a).wait_recv()
+        r["h"][a] = (r["g"][a, my_half, :].astype(F32) + r["pr"][a].astype(F32)).astype(BF16)
         loop(npl - 1, lambda i: rs_copy(a, i + 1).start())
 
     def reduce_middle(a):
         drain(r["rs"].at[a], r["rs_r"].at[a])
-        total = r["g"][a, my_chunk, :].astype(F32)
+        total = r["h"][a, in_half, :].astype(F32)
         for d in range(npl - 1):
             total = total + r["rs"][a, d].astype(F32)
         r["zb"][a, z] = total.astype(BF16)
@@ -474,18 +504,25 @@
         r["fin"][a, my_chunk, :] = total.astype(BF16)
         loop(npl - 1, lambda i: ag_copy(a, i + 1).start())
 
-    def reduce_end(a, layer):
+    def reduce_join(a):
         drain(r["fin"].at[a, 0 : (npl - 1) * chunk, :], r["ag_r"].at[a])
-        pg_out[layer, :, D:] = r["fin"][a, 0:D, :].astype(F32) * factor
-        pg_out[layer, :, 0:D] = r["fin"][a, D:, 0:D].astype(F32) * factor
-        cg_out[layer] = r["fin"][a, D:, D:].astype(F32) * factor
+        join_copy(a).start()
+
+    def fin_copy(a):
+        return pltpu.make_async_copy(r["fin"].at[a], fin_out.at[a], r["out_s"].at[a])
+
+    def reduce_end(a):
+        join_copy(a).wait_recv()
+        fin_copy(a).start()
 
     def reduce_drain(a):
+        pair_copy(a).wait_send()
         drain(r["rs"].at[a], r["rs_s"].at[a])
         drain(r["zb"].at[a, 0 : nz - 1], r["z_s"].at[a])
         drain(r["fin"].at[a, 0 : (npl - 1) * chunk, :], r["ag_s"].at[a])
-
-    reduce_start(0)
+        join_copy(a).wait_send()
+
+    pair_copy(0).start()
 
     r["dkv"][...] = jnp.zeros_like(r["dkv"])
 
@@ -495,25 +532,38 @@
 
     loop(ntm - 1, lambda i: mg_arrival(i + 1).wait_recv())
 
-    for f in range(FR):
-        grad = r["mg"][f]
-        r["do"][f] = nt(grad, r["cv"][0]).astype(BF16)
-        r["dot_t"][:, f * ROWS : (f + 1) * ROWS] = nt(r["cv"][0], grad).astype(BF16)
-
-    def backward_block(f, j):
-        i = 2 * f + j
+    reduce_pair(0)
+    loop(ntm - 1, lambda i: mf_copy(i + 1).start())
+
+    for i in range(4):
+        f, j = i // 2, i % 2
+        turned = nt(r["cv"][0], r["mg"][f, j * BLOCK : (j + 1) * BLOCK, :])
+        share = jnp.broadcast_to(r["share"][i][:, None, :], (HEADS, HD, BLOCK)).reshape(D, BLOCK)
+        turned = turned * share
+        r["delta"][i] = head_sums(r["ot"][i] * turned.astype(BF16).astype(F32))
+        grad = turned.T.astype(BF16)
+        for h in range(HEADS):
+            r["dos"][i, h * BLOCK : (h + 1) * BLOCK, :] = grad * r["hm"][h]
+
+    def edge_copies(f):
+        return [
+            remote(r["dkvb"].at[f, 0:ROWS, :], r["er"].at[f, 1], r["ed_s"].at[f, 0], r["ed_r"].at[f, 0], (tm, left)),
+            remote(
+                r["dkvb"].at[f, 2 * ROWS :, :], r["er"].at[f, 0], r["ed_s"].at[f, 1], r["ed_r"].at[f, 1], (tm, right)
+            ),
+        ]
+
+    def backward_block(i):
+        f = lax.div(i, 2)
+        j = lax.rem(i, 2)
         rows = key_rows(j)
         mine = pl.ds(pl.multiple_of(j * BLOCK, BLOCK), BLOCK)
-        grad = r["do"][f, mine, :]
-        for h in range(HEADS):
-            r["dos"][h * BLOCK : (h + 1) * BLOCK, :] = grad * r["hm"][h]
-        lanes = pl.ds(pl.multiple_of(i * BLOCK, BLOCK), BLOCK)
-        delta = head_sums(r["ot"][i] * r["dot_t"][:, lanes].astype(F32))
+        delta = r["delta"][i]
         outs = []
         for pair in range(HEADS // 2):
             cols = slice(pair * 2 * BLOCK, (pair + 1) * 2 * BLOCK)
             s = r["s"].at[pair % 2]
-            s[...] = nt(r["kv"][f, rows, D:], r["dos"][cols, :])
+            s[...] = nt(r["kv"][f, rows, D:], r["dos"][i, cols, :])
             shift = jnp.concatenate([delta[2 * pair : 2 * pair + 1], delta[2 * pair + 1 : 2 * pair + 2]], axis=1)
             for e in range(SPAN):
                 block = slice(e * BLOCK, (e + 1) * BLOCK)
@@ -521,52 +571,51 @@
             outs.append(diag(nn(r["kvt"][f, pair * 2 * HD : (pair + 1) * 2 * HD, rows], r["ds"][:, cols])))
         r["dq"][f, mine, :] = (jnp.concatenate(outs, axis=0) * SCALE).T.astype(BF16)
         r["dkv"][f, rows, 0:D] += nn(r["ds"][...], r["qs"][i]) * SCALE
-        r["dkv"][f, rows, D:] += nn(r["probs"][i], r["dos"][...])
-
-    def edge_copies(f):
-        return [
-            remote(r["dkvb"].at[f, 0:ROWS, :], r["er"].at[f, 1], r["ed_s"].at[f, 0], r["ed_r"].at[f, 0], (tm, left)),
-            remote(
-                r["dkvb"].at[f, 2 * ROWS :, :], r["er"].at[f, 0], r["ed_s"].at[f, 1], r["ed_r"].at[f, 1], (tm, right)
-            ),
-        ]
-
-    def backward_frame(f):
-        loop(2, lambda j: backward_block(f, j))
-        r["dkvb"][f] = r["dkv"][f].astype(BF16)
-        for item in edge_copies(f):
-            item.start()
-
-    backward_frame(0)
-    reduce_middle(0)
-    backward_frame(1)
-    reduce_share(0)
-
+        r["dkv"][f, rows, D:] += nn(r["probs"][i], r["dos"][i])
+
+        @pl.when(i == 1)
+        def _():
+            r["dkvb"][0] = r["dkv"][0].astype(BF16)
+            for item in edge_copies(0):
+                item.start()
+            reduce_middle(0)
+
+        @pl.when(i == 2)
+        def _():
+            reduce_share(0)
+
+    loop(4, backward_block)
+
+    r["dkvb"][1] = r["dkv"][1].astype(BF16)
     inward = nn(r["act_t"][0], r["dkvb"][0]) + nn(r["act_t"][1], r["dkvb"][1])
     r["g"][1, 0:D, :] = inward.astype(BF16)
     inward = nn(r["act_t"][0, :, ROWS : 2 * ROWS], r["dq"][0]) + nn(r["act_t"][1, :, ROWS : 2 * ROWS], r["dq"][1])
     r["g"][1, D:, 0:D] = inward.astype(BF16)
     outward = nn(r["otb"][:, 0:ROWS], r["mg"][0]) + nn(r["otb"][:, ROWS:], r["mg"][1])
     r["g"][1, D:, D:] = outward.astype(BF16)
-    reduce_start(1)
+    pair_copy(1).start()
+    reduce_pair(1)
+    reduce_middle(1)
+    for item in edge_copies(1):
+        item.start()
+    reduce_join(0)
+    reduce_end(0)
+    reduce_share(1)
 
     for f in range(FR):
         for item in edge_copies(f):
             item.wait_recv()
         pair_grad = r["dkv"][f, ROWS : 2 * ROWS, :] + r["er"][f, 0].astype(F32) + r["er"][f, 1].astype(F32)
         act_grad = nt(r["dq"][f], r["wv"][0, :, 0:D]) + nt(pair_grad.astype(BF16), r["wv"][0, :, D:])
-        fg_out[f] = (r["mg"][f].astype(F32) + norm_back(act_grad, r["nrm"][f], r["rinv"][f])).astype(BF16)
-
-    reduce_middle(1)
-    reduce_end(0, 1)
-    reduce_share(1)
-
-    keep.wait()
+        r["fg"][f] = (r["mg"][f].astype(F32) + norm_back(act_grad, r["nrm"][f], r["rinv"][f])).astype(BF16)
+    field_copy = pltpu.make_async_copy(r["fg"], fg_out, r["out_s"].at[2])
+    field_copy.start()
 
     def mf_arrival(d):
         rows = pl.ds(pl.multiple_of(lax.rem(tm + d, ntm) * part, part), part)
         return remote(r["mfs"].at[d], mixed_out.at[:, rows, :], r["mf_s"].at[d - 1], r["mf_r"].at[d - 1], (tm, sp))
 
+    keep.wait()
     loop(ntm - 1, lambda i: mf_arrival(i + 1).wait_recv())
     loop(ntm - 1, lambda i: mf_copy(i + 1).wait_send())
     loop(ntm - 1, lambda i: mg_copy(i + 1).wait_send())
@@ -579,8 +628,22 @@
         item.wait_send()
     reduce_drain(0)
 
-    reduce_end(1, 0)
+    reduce_join(1)
+    reduce_end(1)
     reduce_drain(1)
+    field_copy.wait()
+    fin_copy(0).wait()
+    fin_copy(1).wait()
+
+
+def finish_kernel(factor, mixed, field, fin, mixed_out, field_out, project_out, combine_out):
+    mixed_out[...] = mixed[...]
+    field_out[...] = field[...]
+    for layer in range(2):
+        part = 1 - layer
+        project_out[layer, :, D:] = fin[part, 0:D, :].astype(F32) * factor
+        project_out[layer, :, 0:D] = fin[part, D:, 0:D].astype(F32) * factor
+        combine_out[layer] = fin[part, D:, D:].astype(F32) * factor
 
 
 def per_device(ntm, nsp, wave_field, cotangent, block_lists, project_weights, combine_weights):
@@ -588,22 +651,31 @@
     names = tuple(shapes)
     anywhere = pl.BlockSpec(memory_space=pl.ANY)
     vmem = pl.BlockSpec(memory_space=pltpu.VMEM)
-    return pl.pallas_call(
+    rows = jax.ShapeDtypeStruct((FR, ROWS, D), BF16)
+    mixed, field, fin = pl.pallas_call(
         functools.partial(step_kernel, ntm, nsp, names),
-        out_shape=(
-            jax.ShapeDtypeStruct((FR, ROWS, D), BF16),
-            jax.ShapeDtypeStruct((FR, ROWS, D), BF16),
-            jax.ShapeDtypeStruct((2, D, 3 * D), F32),
-            jax.ShapeDtypeStruct((2, D, D), F32),
-        ),
+        out_shape=(rows, rows, jax.ShapeDtypeStruct((2, 512, 512), BF16)),
         in_specs=[pl.BlockSpec(memory_space=pltpu.SMEM), anywhere, anywhere, anywhere, anywhere],
-        out_specs=(anywhere, vmem, vmem, vmem),
+        out_specs=(anywhere, anywhere, anywhere),
         scratch_shapes=list(shapes.values()),
         compiler_params=pltpu.CompilerParams(
             collective_id=0, has_side_effects=True, vmem_limit_bytes=60 * 1024 * 1024
         ),
         name="cuboid_step",
     )(block_lists, wave_field, cotangent, project_weights, combine_weights)
+    factor = 1.0 / math.sqrt(FR * ntm * ROWS * nsp)
+    return pl.pallas_call(
+        functools.partial(finish_kernel, factor),
+        out_shape=(
+            rows,
+            rows,
+            jax.ShapeDtypeStruct((2, D, 3 * D), F32),
+            jax.ShapeDtypeStruct((2, D, D), F32),
+        ),
+        in_specs=[vmem] * 3,
+        out_specs=(vmem,) * 4,
+        name="finish",
+    )(mixed, field, fin)
 
 
 def solution(mesh):

time: 107 us -> 84.1 us (0.79)
  Pallas kernels: 99.6 us -> 83.3 us
  local copies, waits for them, and re-layouts: 6.84 us -> 0 us
    pallas_call x1, Pallas kernels: 99.6 us -> 80.4 us  [per_device(): pl.pallas_call(functools.partial(step_kernel, ntm, nsp, names), out_shape...]
    unnamed x6 -> x0, local copies, waits for them, and re-layouts: 6.84 us -> none
    pallas_call x0 -> x1, Pallas kernels: none -> 2.9 us  [per_device(): pl.pallas_call(functools.partial(finish_kernel, factor), out_shape=(rows,...]
where the time goes in v2:
time: 84.1 us; the launch traced here: 83.9 us
  Pallas kernels  83.3 us (99%)
    pallas_call x1, Pallas kernels, per_device(): pl.pallas_call(functools.partial(step_kernel, ntm, nsp, names), out_shape...  80.4 us
    pallas_call x1, Pallas kernels, per_device(): pl.pallas_call(functools.partial(finish_kernel, factor), out_shape=(rows,...  2.9 us

profile of v2, /device:TPU:1, one launch (start us, length us, event | category | flops | bytes accessed | tf_op | source)
XLA Modules:
  0.0 83.9 jit_solution(17614275437329157870)
XLA Ops:
  0.6 80.4 %cuboid_step.1 = (bf16[2,256,256]{2,1,0:T(8,128)(2,1)}, bf16[2,256,256]{2,1,0:T(8,128)(2,1)}, bf16[2,512,512]{2,1,0:T(8,128)(2,1)}) custom-call(s32[2,2,4]{2,1,0:T(2,128)} %lists.1, bf16[2,256,256]{2,1,0:T(8,128)(2,1)} %x_hbm.1, bf16[2,256,256]{2,1,0:T(8,128)(2,1)} %cot_hbm.1, bf16[2,256,768]{2,1,0:T(8,128)(2,1)} %w_hbm.1, bf16[2,256,256]{2,1,0:T(8,128)(2,1)} %c_hbm.1), custom_call_target="tpu_custom_call" | custom-call | tf_op jit(solution)/shard_map/cuboid_step/pallas_call | solution.py:655
  81.0 2.9 %finish.1 = (bf16[2,256,256]{2,1,0:T(8,128)(2,1)}, bf16[2,256,256]{2,1,0:T(8,128)(2,1)}, f32[2,256,768]{2,1,0:T(8,128)}, f32[2,256,256]{2,1,0:T(8,128)}) custom-call(bf16[2,256,256]{2,1,0:T(8,128)(2,1)} %get-tuple-element.7.mixed, bf16[2,256,256]{2,1,0:T(8,128)(2,1)} %get-tuple-element.8.field, bf16[2,512,512]{2,1,0:T(8,128)(2,1)} %get-tuple-element.9.fin), custom_call_target="tpu_custom_call" | custom-call | tf_op jit(solution)/shard_map/finish/pallas_call | solution.py:667

commit v3 on v2

--- a/solution.py
+++ b/solution.py
@@ -20,6 +20,9 @@
 CORES = 4
 EPS = 1e-05
 NEG = -1e30
+PADS = 80
+LIMIT = 60 * 1024 * 1024
+LANES = (512, 256, 128, 128)
 SCALE = 1.0 / math.sqrt(HD)
 SCALE2 = SCALE * math.log2(math.e)
 
@@ -75,14 +78,15 @@
         hm=vm((HEADS, BLOCK, D), BF16),
         q=vm((FR, ROWS, D), BF16),
         kv=vm((FR, 3 * ROWS, 2 * D), BF16),
-        kvt=vm((FR, 2 * D, 3 * ROWS), BF16),
+        kt=vm((FR, D, 3 * ROWS), BF16),
+        vt=vm((FR, HEADS // 2, PADS, 3 * ROWS), BF16),
         qs=vm((4, HEADS * BLOCK, D), BF16),
         dos=vm((4, HEADS * BLOCK, D), BF16),
         share=vm((4, HEADS, BLOCK), F32),
         delta=vm((4, HEADS, BLOCK), F32),
         probs=vm((4, KEYS, HEADS * BLOCK), BF16),
         ds=vm((KEYS, HEADS * BLOCK), BF16),
-        s=vm((2, KEYS, 2 * BLOCK), F32),
+        s=vm((4, KEYS, 2 * BLOCK), F32),
         ot=vm((4, D, BLOCK), F32),
         otb=vm((D, 4 * BLOCK), BF16),
         att=vm((FR, ROWS, D), BF16),
@@ -107,48 +111,57 @@
         tprobs=vm((GROUPS, BLOCK, HEADS * BLOCK), BF16),
         tds=vm((GROUPS, BLOCK, HEADS * BLOCK), BF16),
         tmix=vm((GROUPS, BLOCK, D), F32),
+        tmf=vm((GROUPS, BLOCK, D), F32),
         mfs=vm((ntm, FR, part, D), BF16),
         mgs=vm((ntm, FR, part, D), BF16),
         mg=vm((FR, ROWS, D), BF16),
         dq=vm((FR, ROWS, D), BF16),
         dkv=vm((FR, 3 * ROWS, 2 * D), F32),
         dkvb=vm((FR, 3 * ROWS, 2 * D), BF16),
-        er=vm((FR, 2, ROWS, 2 * D), BF16),
-        g=vm((2, 512, 512), BF16),
-        pr=vm((2, 256, 512), BF16),
-        h=vm((2, 256, 512), BF16),
+        eg=vm((FR, 2, ROWS, D), BF16),
+        er=vm((FR, 2, ROWS, D), BF16),
         fg=vm((FR, ROWS, D), BF16),
-        rs=vm((2, npl - 1, chunk, 512), BF16),
-        zb=vm((2, nz, chunk, 512), BF16),
-        fin=vm((2, 512, 512), BF16),
-        ld_sem=dma((6,)),
-        halo_s=dma((2,)),
-        halo_r=dma((2,)),
+        fgw=vm((FR, ROWS, D), F32),
+        **{
+            name + str(a): vm(shape + (lanes,), BF16)
+            for a, lanes in enumerate(LANES)
+            for name, shape in (
+                ("g", (512,)),
+                ("pr", (256,)),
+                ("h", (256,)),
+                ("rs", (npl - 1, chunk)),
+                ("zb", (nz, chunk)),
+                ("fin", (512,)),
+            )
+        },
+        ld_sem=dma((7,)),
+        halo_s=dma((FR, 2)),
+        halo_r=dma((FR, 2)),
         cot_s=dma((ntm - 1,)),
         cot_r=dma((ntm - 1,)),
         ms_s=dma((FR, ntm - 1)),
         ms_r=dma((FR, ntm - 1)),
         mf_s=dma((ntm - 1,)),
         mf_r=dma((ntm - 1,)),
-        mg_s=dma((ntm - 1,)),
-        mg_r=dma((ntm - 1,)),
+        mg_s=dma((2, ntm - 1)),
+        mg_r=dma((2, ntm - 1)),
         ed_s=dma((FR, 2)),
         ed_r=dma((FR, 2)),
-        pr_s=dma((2,)),
-        pr_r=dma((2,)),
-        pg_s=dma((2,)),
-        pg_r=dma((2,)),
-        out_s=dma((4,)),
-        rs_s=dma((2,)),
-        rs_r=dma((2,)),
-        z_s=dma((2,)),
-        z_r=dma((2,)),
-        ag_s=dma((2,)),
-        ag_r=dma((2,)),
+        pr_s=dma((4,)),
+        pr_r=dma((4,)),
+        pg_s=dma((4,)),
+        pg_r=dma((4,)),
+        out_s=dma((5,)),
+        rs_s=dma((4,)),
+        rs_r=dma((4,)),
+        z_s=dma((4,)),
+        z_r=dma((4,)),
+        ag_s=dma((4,)),
+        ag_r=dma((4,)),
     )
 
 
-def step_kernel(ntm, nsp, names, lists, x_hbm, cot_hbm, w_hbm, c_hbm, mixed_out, fg_out, fin_out, *refs):
+def step_kernel(ntm, nsp, names, lists, x_hbm, cot_hbm, w_hbm, c_hbm, mixed_out, fg_out, fin0_out, fin1_out, fin2_out, fin3_out, *refs):
     r = dict(zip(names, refs))
     nz = nsp // CORES
     npl = ntm * 2
@@ -196,10 +209,11 @@
     own = pl.ds(pl.multiple_of(tm * part, part), part)
     loads = [
         pltpu.make_async_copy(w_hbm.at[0], r["wv"].at[0], ld.at[0]),
-        pltpu.make_async_copy(x_hbm, r["xe"].at[1], ld.at[1]),
+        pltpu.make_async_copy(x_hbm.at[0], r["xe"].at[1, 0], ld.at[1]),
         pltpu.make_async_copy(c_hbm, r["cv"], ld.at[2]),
         pltpu.make_async_copy(w_hbm.at[1], r["wv"].at[1], ld.at[3]),
         pltpu.make_async_copy(cot_hbm.at[:, own, :], r["hcot"].at[0], ld.at[4]),
+        pltpu.make_async_copy(x_hbm.at[1], r["xe"].at[1, 1], ld.at[6]),
     ]
     for item in loads:
         item.start()
@@ -211,17 +225,22 @@
     query_pos = lax.broadcasted_iota(jnp.int32, (BLOCK, 2 * BLOCK), 1) % per
     r["tb"][...] = jnp.where(key_pos == query_pos, 0.0, NEG)
 
+    r["vt"][:, :, 2 * HD :, :] = jnp.ones((FR, HEADS // 2, PADS - 2 * HD, 3 * ROWS), BF16)
+
     loads[0].wait()
     r["wt"][0] = r["wv"][0, :, D:].astype(F32).T.astype(BF16)
 
     pl.semaphore_wait(barrier, 2 + (npl - 1) + (nz - 1))
 
-    halos = [
-        remote(x_hbm, r["xe"].at[2], r["halo_s"].at[0], r["halo_r"].at[0], (tm, left)),
-        remote(x_hbm, r["xe"].at[0], r["halo_s"].at[1], r["halo_r"].at[1], (tm, right)),
-    ]
-    for item in halos:
-        item.start()
+    def halos(f):
+        return [
+            remote(x_hbm.at[f], r["xe"].at[2, f], r["halo_s"].at[f, 0], r["halo_r"].at[f, 0], (tm, left)),
+            remote(x_hbm.at[f], r["xe"].at[0, f], r["halo_s"].at[f, 1], r["halo_r"].at[f, 1], (tm, right)),
+        ]
+
+    for f in range(FR):
+        for item in halos(f):
+            item.start()
 
     def cot_copy(d):
         to = lax.rem(tm + d, ntm)
@@ -240,24 +259,21 @@
             r["rinv"][f] = inverse
             r["q"][f] = nn(act, r["wv"][0, :, 0:D]).astype(BF16)
         r["kv"][f, rows, :] = nn(act, r["wv"][0, :, D:]).astype(BF16)
-        r["kvt"][f, :, rows] = nt(r["wt"][0], act).astype(BF16)
+        turned = nt(r["wt"][0], act).astype(BF16)
+        r["kt"][f, :, rows] = turned[0:D]
+        for pair in range(HEADS // 2):
+            r["vt"][f, pair, 0 : 2 * HD, rows] = turned[D + pair * 2 * HD : D + (pair + 1) * 2 * HD]
 
     loads[1].wait()
-    for f in range(FR):
-        project(1, f)
+    project(1, 0)
+    loads[5].wait()
+    project(1, 1)
     for f in range(FR):
         for j in range(2):
             for h in range(HEADS):
                 r["qs"][2 * f + j, h * BLOCK : (h + 1) * BLOCK, :] = (
                     r["q"][f, j * BLOCK : (j + 1) * BLOCK, :] * r["hm"][h]
                 )
-    halos[0].wait_recv()
-    for f in range(FR):
-        project(2, f)
-    halos[1].wait_recv()
-    loop(ntm - 1, lambda i: cot_copy(i + 1).start())
-    for f in range(FR):
-        project(0, f)
 
     def key_rows(j):
         return pl.ds(pl.multiple_of(j * BLOCK, BLOCK), KEYS)
@@ -283,26 +299,29 @@
         rows = key_rows(j)
         bias = biases(f, j)
         outs = []
+
+        def scores(pair):
+            cols = slice(pair * 2 * BLOCK, (pair + 1) * 2 * BLOCK)
+            r["s"][pair] = nt(r["kv"][f, rows, 0:D], r["qs"][i, cols, :])
+
+        scores(0)
         for pair in range(HEADS // 2):
             cols = slice(pair * 2 * BLOCK, (pair + 1) * 2 * BLOCK)
-            s = r["s"].at[pair % 2]
-            scores = nt(r["kv"][f, rows, 0:D], r["qs"][i, cols, :])
-            s[...] = scores
+            if pair + 1 < HEADS // 2:
+                scores(pair + 1)
+            s = r["s"].at[pair]
             top = None
             for e in range(SPAN):
-                here = jnp.max(scores[e * BLOCK : (e + 1) * BLOCK, :], axis=0, keepdims=True) * SCALE2 + bias[e]
+                here = jnp.max(s[e * BLOCK : (e + 1) * BLOCK, :], axis=0, keepdims=True) * SCALE2 + bias[e]
                 top = here if top is None else jnp.maximum(top, here)
-            total = jnp.zeros((1, 2 * BLOCK), F32)
             for e in range(SPAN):
                 block = slice(e * BLOCK, (e + 1) * BLOCK)
-                grown = jnp.exp2(s[block, :] * SCALE2 + (bias[e] - top))
-                r["probs"][i, block, cols] = grown.astype(BF16)
-                total = total + jnp.sum(grown, axis=0, keepdims=True)
-            share = 1.0 / total
+                r["probs"][i, block, cols] = jnp.exp2(s[block, :] * SCALE2 + (bias[e] - top)).astype(BF16)
+            both = nn(r["vt"][f, pair, :, rows], r["probs"][i, :, cols])
+            share = 1.0 / both[2 * HD : 2 * HD + 1, :]
             r["share"][i, 2 * pair : 2 * pair + 1, :] = share[:, 0:BLOCK]
             r["share"][i, 2 * pair + 1 : 2 * pair + 2, :] = share[:, BLOCK:]
-            values = r["kvt"][f, D + pair * 2 * HD : D + (pair + 1) * 2 * HD, rows]
-            outs.append(diag(nn(values, r["probs"][i, :, cols]) * share))
+            outs.append(diag(both[0 : 2 * HD] * share))
         out = jnp.concatenate(outs, axis=0)
         r["ot"][i] = out
         r["otb"][:, pl.ds(pl.multiple_of(i * BLOCK, BLOCK), BLOCK)] = out.astype(BF16)
@@ -316,13 +335,36 @@
         )
 
     loads[2].wait()
+    half = ntm // 2
 
     def forward_frame(f):
-        loop(2, lambda j: forward_block(f, j))
-        mixed = r["xe"][1, f].astype(F32) + nn(r["att"][f], r["cv"][0])
-        r["ms"][f] = mixed.astype(BF16)
+        for item in halos(f):
+            item.wait_recv()
+
+        @pl.when(f == FR - 1)
+        def _():
+            loop(ntm - 1, lambda i: cot_copy(i + 1).start())
+
+        project(2, f)
+        project(0, f)
+
+        def block(j):
+            forward_block(f, j)
+            rows = pl.ds(pl.multiple_of(j * BLOCK, BLOCK), BLOCK)
+            mixed = r["xe"][1, f, rows, :].astype(F32) + nn(r["att"][f, rows, :], r["cv"][0])
+            r["ms"][f, rows, :] = mixed.astype(BF16)
+
+            def send(i):
+                to = j * half + i
+
+                @pl.when(to != tm)
+                def _():
+                    ms_copy(f, lax.rem(to - tm + ntm, ntm)).start()
+
+            loop(half, send)
+
+        loop(2, block)
         r["hist"][0, f] = r["ms"][f, own, :]
-        loop(ntm - 1, lambda i: ms_copy(f, i + 1).start())
 
     loop(FR, forward_frame)
 
@@ -342,12 +384,12 @@
                 for g in range(GROUPS):
                     dst[g, frame * per : (frame + 1) * per, :] = rows[g * per : (g + 1) * per]
 
-    def ungroup(src, dst):
+    def ungroup(src, dst, side):
         for d in range(ntm):
             for f in range(FR):
                 frame = d * FR + f
-                dst[d, f] = jnp.concatenate(
-                    [src[g, frame * per : (frame + 1) * per, :] for g in range(GROUPS)], axis=0
+                dst[d, f, side * 2 * per : (side + 1) * 2 * per, :] = jnp.concatenate(
+                    [src[g, frame * per : (frame + 1) * per, :] for g in (2 * side, 2 * side + 1)], axis=0
                 ).astype(BF16)
 
     regroup(r["hcot"], r["ct"])
@@ -419,13 +461,12 @@
         time_scores(g)
     for g in range(GROUPS):
         time_out(g)
-    for g in range(GROUPS):
-        time_grads(g)
-
-    def mg_copy(d):
+    def mg_copy(d, side):
+        from_rows = pl.ds(side * 2 * per, 2 * per)
+        to_rows = pl.ds(pl.multiple_of(tm * part + side * 2 * per, 2 * per), 2 * per)
         return remote(
-            r["mgs"].at[d], r["mg"].at[:, own, :], r["mg_s"].at[d - 1], r["mg_r"].at[d - 1],
-            (lax.rem(tm + (ntm - d), ntm), sp),
+            r["mgs"].at[d, :, from_rows, :], r["mg"].at[:, to_rows, :], r["mg_s"].at[side, d - 1],
+            r["mg_r"].at[side, d - 1], (lax.rem(tm + (ntm - d), ntm), sp),
         )
 
     def mf_copy(d):
@@ -434,26 +475,30 @@
             (lax.rem(tm + (ntm - d), ntm), sp),
         )
 
+    for side in range(2):
+        for g in (2 * side, 2 * side + 1):
+            time_grads(g)
+        for g in (2 * side, 2 * side + 1):
+            rows = slice(g * BLOCK, (g + 1) * BLOCK)
+            act_grad = nt(r["tdp"][rows, :], r["wv"][1])
+            r["tmix"][g] = r["ct"][g] + norm_back(act_grad, r["tnrm"][rows, :], r["trinv"][rows, :])
+        ungroup(r["tmix"], r["mgs"], side)
+        loop(ntm - 1, lambda i, side=side: mg_copy(i + 1, side).start())
+    r["mg"][:, own, :] = r["mgs"][0]
+
     for g in range(GROUPS):
         rows = slice(g * BLOCK, (g + 1) * BLOCK)
-        act_grad = nt(r["tdp"][rows, :], r["wv"][1])
-        r["tmix"][g] = r["ct"][g] + norm_back(act_grad, r["tnrm"][rows, :], r["trinv"][rows, :])
-    ungroup(r["tmix"], r["mgs"])
-    loop(ntm - 1, lambda i: mg_copy(i + 1).start())
-    r["mg"][:, own, :] = r["mgs"][0]
-
-    for g in range(GROUPS):
-        rows = slice(g * BLOCK, (g + 1) * BLOCK)
-        r["tmix"][g] = r["xt"][g] + nn(r["tatt"][rows, :], r["cv"][1])
-    ungroup(r["tmix"], r["mfs"])
+        r["tmf"][g] = r["xt"][g] + nn(r["tatt"][rows, :], r["cv"][1])
+    for side in range(2):
+        ungroup(r["tmf"], r["mfs"], side)
     keep = pltpu.make_async_copy(r["mfs"].at[0], mixed_out.at[:, own, :], ld.at[5])
     keep.start()
 
     turned = r["tact"][...].astype(F32).T.astype(BF16)
-    r["g"][0, 0:D, :] = nn(turned, r["tdp"][:, D:]).astype(BF16)
-    r["g"][0, D:, 0:D] = nn(turned, r["tdp"][:, 0:D]).astype(BF16)
+    r["g0"][0:D, :] = nn(turned, r["tdp"][:, D:]).astype(BF16)
+    r["g0"][D:, 0:D] = nn(turned, r["tdp"][:, 0:D]).astype(BF16)
     cots = r["ct"][...].reshape(GROUPS * BLOCK, D).astype(BF16)
-    r["g"][0, D:, D:] = nn(r["tot"][...], cots).astype(BF16)
+    r["g0"][D:, D:] = nn(r["tot"][...], cots).astype(BF16)
 
     my_half = pl.ds(pl.multiple_of(core * 256, 256), 256)
     other_half = pl.ds(pl.multiple_of((1 - core) * 256, 256), 256)
@@ -461,23 +506,23 @@
     my_chunk = pl.ds(pl.multiple_of(core * 256 + place * chunk, chunk), chunk)
 
     def pair_copy(a):
-        return remote(r["g"].at[a, other_half, :], r["pr"].at[a], r["pr_s"].at[a], r["pr_r"].at[a], (tm, partner))
+        return remote(r["g" + str(a)].at[other_half, :], r["pr" + str(a)], r["pr_s"].at[a], r["pr_r"].at[a], (tm, partner))
 
     def rs_copy(a, d):
         device, other = plane_peer(d)
         rows = pl.ds(pl.multiple_of(other * chunk, chunk), chunk)
-        return remote(r["h"].at[a, rows, :], r["rs"].at[a, d - 1], r["rs_s"].at[a], r["rs_r"].at[a], device)
+        return remote(r["h" + str(a)].at[rows, :], r["rs" + str(a)].at[d - 1], r["rs_s"].at[a], r["rs_r"].at[a], device)
 
     def z_copy(a, d):
-        return remote(r["zb"].at[a, z], r["zb"].at[a, z], r["z_s"].at[a], r["z_r"].at[a], z_peer(d))
+        return remote(r["zb" + str(a)].at[z], r["zb" + str(a)].at[z], r["z_s"].at[a], r["z_r"].at[a], z_peer(d))
 
     def ag_copy(a, d):
         device, _ = plane_peer(d)
-        return remote(r["fin"].at[a, my_chunk, :], r["fin"].at[a, my_chunk, :], r["ag_s"].at[a], r["ag_r"].at[a], device)
+        return remote(r["fin" + str(a)].at[my_chunk, :], r["fin" + str(a)].at[my_chunk, :], r["ag_s"].at[a], r["ag_r"].at[a], device)
 
     def join_copy(a):
         return remote(
-            r["fin"].at[a, my_half, :], r["fin"].at[a, my_half, :], r["pg_s"].at[a], r["pg_r"].at[a], (tm, partner)
+            r["fin" + str(a)].at[my_half, :], r["fin" + str(a)].at[my_half, :], r["pg_s"].at[a], r["pg_r"].at[a], (tm, partner)
         )
 
     def drain(ref, sem):
@@ -485,31 +530,31 @@
 
     def reduce_pair(a):
         pair_copy(a).wait_recv()
-        r["h"][a] = (r["g"][a, my_half, :].astype(F32) + r["pr"][a].astype(F32)).astype(BF16)
+        r["h" + str(a)][...] = (r["g" + str(a)][my_half, :].astype(F32) + r["pr" + str(a)][...].astype(F32)).astype(BF16)
         loop(npl - 1, lambda i: rs_copy(a, i + 1).start())
 
     def reduce_middle(a):
-        drain(r["rs"].at[a], r["rs_r"].at[a])
-        total = r["h"][a, in_half, :].astype(F32)
+        drain(r["rs" + str(a)], r["rs_r"].at[a])
+        total = r["h" + str(a)][in_half, :].astype(F32)
         for d in range(npl - 1):
-            total = total + r["rs"][a, d].astype(F32)
-        r["zb"][a, z] = total.astype(BF16)
+            total = total + r["rs" + str(a)][d].astype(F32)
+        r["zb" + str(a)][z] = total.astype(BF16)
         loop(nz - 1, lambda i: z_copy(a, i + 1).start())
 
     def reduce_share(a):
-        drain(r["zb"].at[a, 0 : nz - 1], r["z_r"].at[a])
-        total = r["zb"][a, 0].astype(F32)
+        drain(r["zb" + str(a)].at[0 : nz - 1], r["z_r"].at[a])
+        total = r["zb" + str(a)][0].astype(F32)
         for k in range(1, nz):
-            total = total + r["zb"][a, k].astype(F32)
-        r["fin"][a, my_chunk, :] = total.astype(BF16)
+            total = total + r["zb" + str(a)][k].astype(F32)
+        r["fin" + str(a)][my_chunk, :] = total.astype(BF16)
         loop(npl - 1, lambda i: ag_copy(a, i + 1).start())
 
     def reduce_join(a):
-        drain(r["fin"].at[a, 0 : (npl - 1) * chunk, :], r["ag_r"].at[a])
+        drain(r["fin" + str(a)].at[0 : (npl - 1) * chunk, :], r["ag_r"].at[a])
         join_copy(a).start()
 
     def fin_copy(a):
-        return pltpu.make_async_copy(r["fin"].at[a], fin_out.at[a], r["out_s"].at[a])
+        return pltpu.make_async_copy(r["fin" + str(a)], (fin0_out, fin1_out, fin2_out, fin3_out)[a], r["out_s"].at[a])
 
     def reduce_end(a):
         join_copy(a).wait_recv()
@@ -517,23 +562,31 @@
 
     def reduce_drain(a):
         pair_copy(a).wait_send()
-        drain(r["rs"].at[a], r["rs_s"].at[a])
-        drain(r["zb"].at[a, 0 : nz - 1], r["z_s"].at[a])
-        drain(r["fin"].at[a, 0 : (npl - 1) * chunk, :], r["ag_s"].at[a])
+        drain(r["rs" + str(a)], r["rs_s"].at[a])
+        drain(r["zb" + str(a)].at[0 : nz - 1], r["z_s"].at[a])
+        drain(r["fin" + str(a)].at[0 : (npl - 1) * chunk, :], r["ag_s"].at[a])
         join_copy(a).wait_send()
 
     pair_copy(0).start()
 
     r["dkv"][...] = jnp.zeros_like(r["dkv"])
 
-    def mg_arrival(d):
-        rows = pl.ds(pl.multiple_of(lax.rem(tm + d, ntm) * part, part), part)
-        return remote(r["mgs"].at[d], r["mg"].at[:, rows, :], r["mg_s"].at[d - 1], r["mg_r"].at[d - 1], (tm, sp))
-
-    loop(ntm - 1, lambda i: mg_arrival(i + 1).wait_recv())
-
+    def mg_arrival(d, side):
+        rows = pl.ds(pl.multiple_of(lax.rem(tm + d, ntm) * part + side * 2 * per, 2 * per), 2 * per)
+        from_rows = pl.ds(side * 2 * per, 2 * per)
+        return remote(
+            r["mgs"].at[d, :, from_rows, :], r["mg"].at[:, rows, :], r["mg_s"].at[side, d - 1],
+            r["mg_r"].at[side, d - 1], (tm, sp),
+        )
+
+    for side in range(2):
+        loop(ntm - 1, lambda i, side=side: mg_arrival(i + 1, side).wait_recv())
+
+    outward = nn(r["otb"][:, 0:ROWS], r["mg"][0]) + nn(r["otb"][:, ROWS:], r["mg"][1])
+    r["g2"][0:D, :] = outward[:, 0:BLOCK].astype(BF16)
+    r["g2"][D:, :] = outward[:, BLOCK:].astype(BF16)
+    pair_copy(2).start()
     reduce_pair(0)
-    loop(ntm - 1, lambda i: mf_copy(i + 1).start())
 
     for i in range(4):
         f, j = i // 2, i % 2
@@ -545,13 +598,17 @@
         for h in range(HEADS):
             r["dos"][i, h * BLOCK : (h + 1) * BLOCK, :] = grad * r["hm"][h]
 
-    def edge_copies(f):
-        return [
-            remote(r["dkvb"].at[f, 0:ROWS, :], r["er"].at[f, 1], r["ed_s"].at[f, 0], r["ed_r"].at[f, 0], (tm, left)),
-            remote(
-                r["dkvb"].at[f, 2 * ROWS :, :], r["er"].at[f, 0], r["ed_s"].at[f, 1], r["ed_r"].at[f, 1], (tm, right)
-            ),
-        ]
+    def edge_copy(f, side):
+        return remote(
+            r["eg"].at[f, side], r["er"].at[f, 1 - side], r["ed_s"].at[f, side], r["ed_r"].at[f, side],
+            (tm, right if side else left),
+        )
+
+    def edge_send(f):
+        for side in range(2):
+            rows = slice(2 * ROWS * side, 2 * ROWS * side + ROWS)
+            r["eg"][f, side] = nt(r["dkvb"][f, rows, :], r["wv"][0, :, D:]).astype(BF16)
+            edge_copy(f, side).start()
 
     def backward_block(i):
         f = lax.div(i, 2)
@@ -560,55 +617,72 @@
         mine = pl.ds(pl.multiple_of(j * BLOCK, BLOCK), BLOCK)
         delta = r["delta"][i]
         outs = []
+
+        def grads(pair):
+            cols = slice(pair * 2 * BLOCK, (pair + 1) * 2 * BLOCK)
+            r["s"][pair] = nt(r["kv"][f, rows, D:], r["dos"][i, cols, :])
+
+        grads(0)
         for pair in range(HEADS // 2):
             cols = slice(pair * 2 * BLOCK, (pair + 1) * 2 * BLOCK)
-            s = r["s"].at[pair % 2]
-            s[...] = nt(r["kv"][f, rows, D:], r["dos"][i, cols, :])
+            s = r["s"].at[pair]
+            if pair + 1 < HEADS // 2:
+                grads(pair + 1)
             shift = jnp.concatenate([delta[2 * pair : 2 * pair + 1], delta[2 * pair + 1 : 2 * pair + 2]], axis=1)
             for e in range(SPAN):
                 block = slice(e * BLOCK, (e + 1) * BLOCK)
                 r["ds"][block, cols] = (r["probs"][i, block, cols].astype(F32) * (s[block, :] - shift)).astype(BF16)
-            outs.append(diag(nn(r["kvt"][f, pair * 2 * HD : (pair + 1) * 2 * HD, rows], r["ds"][:, cols])))
+            outs.append(diag(nn(r["kt"][f, pair * 2 * HD : (pair + 1) * 2 * HD, rows], r["ds"][:, cols])))
         r["dq"][f, mine, :] = (jnp.concatenate(outs, axis=0) * SCALE).T.astype(BF16)
         r["dkv"][f, rows, 0:D] += nn(r["ds"][...], r["qs"][i]) * SCALE
         r["dkv"][f, rows, D:] += nn(r["probs"][i], r["dos"][i])
 
+        @pl.when(i == 0)
+        def _():
+            reduce_pair(2)
+
         @pl.when(i == 1)
         def _():
             r["dkvb"][0] = r["dkv"][0].astype(BF16)
-            for item in edge_copies(0):
-                item.start()
-            reduce_middle(0)
+            edge_send(0)
+            loop(ntm - 1, lambda k: mf_copy(k + 1).start())
 
         @pl.when(i == 2)
         def _():
-            reduce_share(0)
+            reduce_middle(0)
+            reduce_middle(2)
 
     loop(4, backward_block)
 
+    inward = nn(r["act_t"][0, :, ROWS : 2 * ROWS], r["dq"][0]) + nn(r["act_t"][1, :, ROWS : 2 * ROWS], r["dq"][1])
+    r["g3"][0:D, :] = inward[:, 0:BLOCK].astype(BF16)
+    r["g3"][D:, :] = inward[:, BLOCK:].astype(BF16)
+    pair_copy(3).start()
     r["dkvb"][1] = r["dkv"][1].astype(BF16)
     inward = nn(r["act_t"][0], r["dkvb"][0]) + nn(r["act_t"][1], r["dkvb"][1])
-    r["g"][1, 0:D, :] = inward.astype(BF16)
-    inward = nn(r["act_t"][0, :, ROWS : 2 * ROWS], r["dq"][0]) + nn(r["act_t"][1, :, ROWS : 2 * ROWS], r["dq"][1])
-    r["g"][1, D:, 0:D] = inward.astype(BF16)
-    outward = nn(r["otb"][:, 0:ROWS], r["mg"][0]) + nn(r["otb"][:, ROWS:], r["mg"][1])
-    r["g"][1, D:, D:] = outward.astype(BF16)
+    r["g1"][0:D, :] = inward[:, 0:D].astype(BF16)
+    r["g1"][D:, :] = inward[:, D:].astype(BF16)
     pair_copy(1).start()
+    reduce_pair(3)
     reduce_pair(1)
+    edge_send(1)
+    for f in range(FR):
+        r["fgw"][f] = nt(r["dq"][f], r["wv"][0, :, 0:D]) + nt(r["dkvb"][f, ROWS : 2 * ROWS, :], r["wv"][0, :, D:])
+    reduce_share(0)
+    reduce_share(2)
+    reduce_middle(3)
     reduce_middle(1)
-    for item in edge_copies(1):
-        item.start()
-    reduce_join(0)
-    reduce_end(0)
+    reduce_share(3)
     reduce_share(1)
+    for a in (0, 2):
+        reduce_join(a)
 
     for f in range(FR):
-        for item in edge_copies(f):
-            item.wait_recv()
-        pair_grad = r["dkv"][f, ROWS : 2 * ROWS, :] + r["er"][f, 0].astype(F32) + r["er"][f, 1].astype(F32)
-        act_grad = nt(r["dq"][f], r["wv"][0, :, 0:D]) + nt(pair_grad.astype(BF16), r["wv"][0, :, D:])
+        for side in range(2):
+            edge_copy(f, side).wait_recv()
+        act_grad = r["fgw"][f] + r["er"][f, 0].astype(F32) + r["er"][f, 1].astype(F32)
         r["fg"][f] = (r["mg"][f].astype(F32) + norm_back(act_grad, r["nrm"][f], r["rinv"][f])).astype(BF16)
-    field_copy = pltpu.make_async_copy(r["fg"], fg_out, r["out_s"].at[2])
+    field_copy = pltpu.make_async_copy(r["fg"], fg_out, r["out_s"].at[4])
     field_copy.start()
 
     def mf_arrival(d):
@@ -618,32 +692,43 @@
     keep.wait()
     loop(ntm - 1, lambda i: mf_arrival(i + 1).wait_recv())
     loop(ntm - 1, lambda i: mf_copy(i + 1).wait_send())
-    loop(ntm - 1, lambda i: mg_copy(i + 1).wait_send())
+    for side in range(2):
+        loop(ntm - 1, lambda i, side=side: mg_copy(i + 1, side).wait_send())
     loop(ntm - 1, lambda i: cot_copy(i + 1).wait_send())
     for f in range(FR):
         loop(ntm - 1, lambda i, f=f: ms_copy(f, i + 1).wait_send())
-        for item in edge_copies(f):
+        for side in range(2):
+            edge_copy(f, side).wait_send()
+        for item in halos(f):
             item.wait_send()
-    for item in halos:
-        item.wait_send()
     reduce_drain(0)
-
+    reduce_drain(2)
+
+    for a in (0, 2):
+        reduce_end(a)
+    reduce_join(3)
     reduce_join(1)
+    reduce_end(3)
     reduce_end(1)
+    reduce_drain(3)
     reduce_drain(1)
     field_copy.wait()
-    fin_copy(0).wait()
-    fin_copy(1).wait()
-
-
-def finish_kernel(factor, mixed, field, fin, mixed_out, field_out, project_out, combine_out):
+    for a in range(4):
+        fin_copy(a).wait()
+
+
+def finish_kernel(factor, mixed, field, fin0, fin1, fin2, fin3, mixed_out, field_out, project_out, combine_out):
     mixed_out[...] = mixed[...]
     field_out[...] = field[...]
-    for layer in range(2):
-        part = 1 - layer
-        project_out[layer, :, D:] = fin[part, 0:D, :].astype(F32) * factor
-        project_out[layer, :, 0:D] = fin[part, D:, 0:D].astype(F32) * factor
-        combine_out[layer] = fin[part, D:, D:].astype(F32) * factor
+    project_out[1, :, D:] = fin0[0:D, :].astype(F32) * factor
+    project_out[1, :, 0:D] = fin0[D:, 0:D].astype(F32) * factor
+    combine_out[1] = fin0[D:, D:].astype(F32) * factor
+    project_out[0, :, 0:BLOCK] = fin3[0:D, :].astype(F32) * factor
+    project_out[0, :, BLOCK:D] = fin3[D:, :].astype(F32) * factor
+    project_out[0, :, D : 2 * D] = fin1[0:D, :].astype(F32) * factor
+    project_out[0, :, 2 * D :] = fin1[D:, :].astype(F32) * factor
+    combine_out[0, :, 0:BLOCK] = fin2[0:D, :].astype(F32) * factor
+    combine_out[0, :, BLOCK:] = fin2[D:, :].astype(F32) * factor
 
 
 def per_device(ntm, nsp, wave_field, cotangent, block_lists, project_weights, combine_weights):
@@ -652,14 +737,14 @@
     anywhere = pl.BlockSpec(memory_space=pl.ANY)
     vmem = pl.BlockSpec(memory_space=pltpu.VMEM)
     rows = jax.ShapeDtypeStruct((FR, ROWS, D), BF16)
-    mixed, field, fin = pl.pallas_call(
+    results = pl.pallas_call(
         functools.partial(step_kernel, ntm, nsp, names),
-        out_shape=(rows, rows, jax.ShapeDtypeStruct((2, 512, 512), BF16)),
+        out_shape=(rows, rows) + tuple(jax.ShapeDtypeStruct((512, lanes), BF16) for lanes in LANES),
         in_specs=[pl.BlockSpec(memory_space=pltpu.SMEM), anywhere, anywhere, anywhere, anywhere],
-        out_specs=(anywhere, anywhere, anywhere),
+        out_specs=(anywhere,) * 6,
         scratch_shapes=list(shapes.values()),
         compiler_params=pltpu.CompilerParams(
-            collective_id=0, has_side_effects=True, vmem_limit_bytes=60 * 1024 * 1024
+            collective_id=0, has_side_effects=True, vmem_limit_bytes=LIMIT
         ),
         name="cuboid_step",
     )(block_lists, wave_field, cotangent, project_weights, combine_weights)
@@ -672,10 +757,10 @@
             jax.ShapeDtypeStruct((2, D, 3 * D), F32),
             jax.ShapeDtypeStruct((2, D, D), F32),
         ),
-        in_specs=[vmem] * 3,
+        in_specs=[vmem] * 6,
         out_specs=(vmem,) * 4,
         name="finish",
-    )(mixed, field, fin)
+    )(*results)
 
 
 def solution(mesh):

time: 84.1 us -> 72.4 us (0.86)
  Pallas kernels: 83.3 us -> 71.6 us
    pallas_call x1, Pallas kernels: 80.4 us -> 68.8 us  [per_device(): pl.pallas_call(functools.partial(step_kernel, ntm, nsp, names), out_shape...]
where the time goes in v3:
time: 72.4 us; the launch traced here: 72.3 us
  Pallas kernels  71.6 us (99%)
    pallas_call x1, Pallas kernels, per_device(): pl.pallas_call(functools.partial(step_kernel, ntm, nsp, names), out_shape...  68.8 us
    pallas_call x1, Pallas kernels, per_device(): pl.pallas_call(functools.partial(finish_kernel, factor), out_shape=(rows,...  2.84 us

profile of v3, /device:TPU:1, one launch (start us, length us, event | category | flops | bytes accessed | tf_op | source)
XLA Modules:
  0.0 72.3 jit_solution(13315023441465836446)
XLA Ops:
  0.6 68.8 %cuboid_step.1 = (bf16[2,256,256]{2,1,0:T(8,128)(2,1)}, bf16[2,256,256]{2,1,0:T(8,128)(2,1)}, bf16[512,512]{1,0:T(8,128)(2,1)}, bf16[512,256]{1,0:T(8,128)(2,1)}...) custom-call(s32[2,2,4]{2,1,0:T(2,128)} %lists.1, bf16[2,256,256]{2,1,0:T(8,128)(2,1)} %x_hbm.1, ...), custom_call_target="tpu_custom_call" | custom-call | tf_op jit(solution)/shard_map/cuboid_step/pallas_call | solution.py:740
  69.4 2.8 %finish.1 = (bf16[2,256,256]{2,1,0:T(8,128)(2,1)}, bf16[2,256,256]{2,1,0:T(8,128)(2,1)}, f32[2,256,768]{2,1,0:T(8,128)}, f32[2,256,256]{2,1,0:T(8,128)}) custom-call(bf16[2,256,256]{2,1,0:T(8,128)(2,1)} %get-tuple-element.10.mixed, bf16[2,256,256]{2,1,0:T(8,128)(2,1)} %get-tuple-element.11.field, bf16[512,512]{1,0:T(8,128)(2,1)} %get-tuple-element.12.fin0, ...), custom_call_target="tpu_custom_call" | custom-call | tf_op jit(solution)/shard_map/finish/pallas_call | solution.py:752

commit v4 on v3

--- a/solution.py
+++ b/solution.py
@@ -131,18 +131,20 @@
                 ("h", (256,)),
                 ("rs", (npl - 1, chunk)),
                 ("zb", (nz, chunk)),
-                ("fin", (512,)),
+                ("fin", (chunk,)),
             )
         },
-        ld_sem=dma((7,)),
+        lists=pltpu.SMEM((FR, 2, 4), jnp.int32),
+        ld_sem=dma((8,)),
+        own_sem=dma((2, 2)),
         halo_s=dma((FR, 2)),
         halo_r=dma((FR, 2)),
-        cot_s=dma((ntm - 1,)),
-        cot_r=dma((ntm - 1,)),
-        ms_s=dma((FR, ntm - 1)),
-        ms_r=dma((FR, ntm - 1)),
-        mf_s=dma((ntm - 1,)),
-        mf_r=dma((ntm - 1,)),
+        cot_s=dma((2, ntm - 1)),
+        cot_r=dma((2, ntm - 1)),
+        ms_s=dma((2, FR, ntm - 1)),
+        ms_r=dma((2, FR, ntm - 1)),
+        mf_s=dma((2, ntm - 1)),
+        mf_r=dma((2, ntm - 1)),
         mg_s=dma((2, ntm - 1)),
         mg_r=dma((2, ntm - 1)),
         ed_s=dma((FR, 2)),
@@ -161,11 +163,11 @@
     )
 
 
-def step_kernel(ntm, nsp, names, lists, x_hbm, cot_hbm, w_hbm, c_hbm, mixed_out, fg_out, fin0_out, fin1_out, fin2_out, fin3_out, *refs):
+def step_kernel(ntm, nsp, names, lists_hbm, x_hbm, cot_hbm, w_hbm, c_hbm, mixed_out, fg_out, fin0_out, fin1_out, fin2_out, fin3_out, *refs):
     r = dict(zip(names, refs))
     nz = nsp // CORES
     npl = ntm * 2
-    part = ROWS // ntm
+    hp = ROWS // ntm // 2
     chunk = 256 // npl
     frames = FR * ntm
     per = BLOCK // frames
@@ -206,14 +208,26 @@
     loop(nz - 1, lambda i: pl.semaphore_signal(barrier, inc=1, device_id=z_peer(i + 1), device_id_type=MESH))
 
     ld = r["ld_sem"]
-    own = pl.ds(pl.multiple_of(tm * part, part), part)
+
+    def side_rows(device, side):
+        return pl.ds(pl.multiple_of(side * BLOCK + device * hp, hp), hp)
+
+    def in_part(side):
+        return pl.ds(side * hp, hp)
+
     loads = [
         pltpu.make_async_copy(w_hbm.at[0], r["wv"].at[0], ld.at[0]),
         pltpu.make_async_copy(x_hbm.at[0], r["xe"].at[1, 0], ld.at[1]),
         pltpu.make_async_copy(c_hbm, r["cv"], ld.at[2]),
         pltpu.make_async_copy(w_hbm.at[1], r["wv"].at[1], ld.at[3]),
-        pltpu.make_async_copy(cot_hbm.at[:, own, :], r["hcot"].at[0], ld.at[4]),
+        pltpu.make_async_copy(
+            cot_hbm.at[:, side_rows(tm, 0), :], r["hcot"].at[0, :, in_part(0), :], r["own_sem"].at[0, 0]
+        ),
         pltpu.make_async_copy(x_hbm.at[1], r["xe"].at[1, 1], ld.at[6]),
+        pltpu.make_async_copy(lists_hbm, r["lists"], ld.at[7]),
+        pltpu.make_async_copy(
+            cot_hbm.at[:, side_rows(tm, 1), :], r["hcot"].at[0, :, in_part(1), :], r["own_sem"].at[0, 1]
+        ),
     ]
     for item in loads:
         item.start()
@@ -242,11 +256,11 @@
         for item in halos(f):
             item.start()
 
-    def cot_copy(d):
+    def cot_copy(d, side):
         to = lax.rem(tm + d, ntm)
-        rows = pl.ds(pl.multiple_of(to * part, part), part)
         return remote(
-            cot_hbm.at[:, rows, :], r["hcot"].at[d], r["cot_s"].at[d - 1], r["cot_r"].at[d - 1], (to, sp)
+            cot_hbm.at[:, side_rows(to, side), :], r["hcot"].at[d, :, in_part(side), :], r["cot_s"].at[side, d - 1],
+            r["cot_r"].at[side, d - 1], (to, sp),
         )
 
     def project(slot, f):
@@ -284,7 +298,7 @@
         for e in range(SPAN):
             count = jnp.int32(0)
             for k in range(4):
-                count = count + jnp.where(lists[f, j, k] == first + e, 1, 0)
+                count = count + jnp.where(r["lists"][f, j, k] == first + e, 1, 0)
             out.append(
                 jnp.where(
                     count == 0,
@@ -327,62 +341,48 @@
         r["otb"][:, pl.ds(pl.multiple_of(i * BLOCK, BLOCK), BLOCK)] = out.astype(BF16)
         r["att"][f, pl.ds(pl.multiple_of(j * BLOCK, BLOCK), BLOCK), :] = out.T.astype(BF16)
 
-    def ms_copy(f, d):
+    def ms_copy(f, side, d):
         to = lax.rem(tm + d, ntm)
-        rows = pl.ds(pl.multiple_of(to * part, part), part)
         return remote(
-            r["ms"].at[f, rows, :], r["hist"].at[d, f], r["ms_s"].at[f, d - 1], r["ms_r"].at[f, d - 1], (to, sp)
+            r["ms"].at[f, side_rows(to, side), :],
+            r["hist"].at[d, f, pl.ds(pl.multiple_of(side * hp, hp), hp), :],
+            r["ms_s"].at[side, f, d - 1],
+            r["ms_r"].at[side, f, d - 1],
+            (to, sp),
         )
 
-    loads[2].wait()
-    half = ntm // 2
-
-    def forward_frame(f):
-        for item in halos(f):
-            item.wait_recv()
-
-        @pl.when(f == FR - 1)
-        def _():
-            loop(ntm - 1, lambda i: cot_copy(i + 1).start())
-
-        project(2, f)
-        project(0, f)
-
-        def block(j):
-            forward_block(f, j)
-            rows = pl.ds(pl.multiple_of(j * BLOCK, BLOCK), BLOCK)
-            mixed = r["xe"][1, f, rows, :].astype(F32) + nn(r["att"][f, rows, :], r["cv"][0])
-            r["ms"][f, rows, :] = mixed.astype(BF16)
-
-            def send(i):
-                to = j * half + i
-
-                @pl.when(to != tm)
-                def _():
-                    ms_copy(f, lax.rem(to - tm + ntm, ntm)).start()
-
-            loop(half, send)
-
-        loop(2, block)
-        r["hist"][0, f] = r["ms"][f, own, :]
-
-    loop(FR, forward_frame)
-
-    for f in range(FR):
-        for slot in range(3):
-            r["act_t"][f, :, slot * ROWS : (slot + 1) * ROWS] = r["act"][slot, f].astype(F32).T.astype(BF16)
     loads[3].wait()
     r["wt"][1] = r["wv"][1, :, D:].astype(F32).T.astype(BF16)
-    loads[4].wait()
-    loop(ntm - 1, lambda i: cot_copy(i + 1).wait_recv())
-
-    def regroup(src, dst):
-        for d in range(ntm):
-            for f in range(FR):
-                frame = d * FR + f
-                rows = src[d, f].astype(F32)
-                for g in range(GROUPS):
-                    dst[g, frame * per : (frame + 1) * per, :] = rows[g * per : (g + 1) * per]
+    loads[2].wait()
+    loads[6].wait()
+
+    def forward(o):
+        f = lax.rem(o, FR)
+        j = lax.div(o, FR)
+
+        @pl.when(j == 0)
+        def _():
+            for item in halos(f):
+                item.wait_recv()
+
+        @pl.when(o == FR - 1)
+        def _():
+            for side in range(2):
+                loop(ntm - 1, lambda i, side=side: cot_copy(i + 1, side).start())
+
+        @pl.when(j == 0)
+        def _():
+            project(2, f)
+            project(0, f)
+
+        forward_block(f, j)
+        rows = pl.ds(pl.multiple_of(j * BLOCK, BLOCK), BLOCK)
+        mixed = r["xe"][1, f, rows, :].astype(F32) + nn(r["att"][f, rows, :], r["cv"][0])
+        r["ms"][f, rows, :] = mixed.astype(BF16)
+        loop(ntm - 1, lambda i: ms_copy(f, j, i + 1).start())
+        r["hist"][0, f, pl.ds(pl.multiple_of(j * hp, hp), hp), :] = r["ms"][f, side_rows(tm, j), :]
+
+    loop(2 * FR, forward)
 
     def ungroup(src, dst, side):
         for d in range(ntm):
@@ -392,31 +392,41 @@
                     [src[g, frame * per : (frame + 1) * per, :] for g in (2 * side, 2 * side + 1)], axis=0
                 ).astype(BF16)
 
-    regroup(r["hcot"], r["ct"])
-    for g in range(GROUPS):
-        rows = slice(g * BLOCK, (g + 1) * BLOCK)
-        cot = r["ct"][g].astype(BF16)
-        grad = nt(cot, r["cv"][1]).astype(BF16)
-        for h in range(HEADS):
-            r["tdos"][g, h * BLOCK : (h + 1) * BLOCK, :] = grad * r["hm"][h]
-        r["tdot"][:, rows] = nt(r["cv"][1], cot).astype(BF16)
-
-    for f in range(FR):
-        loop(ntm - 1, lambda i, f=f: ms_copy(f, i + 1).wait_recv())
+    def time_inputs(side):
+        mine = slice(side * hp, (side + 1) * hp)
+        groups = (2 * side, 2 * side + 1)
+        loads[(4, 7)[side]].wait()
+        loop(ntm - 1, lambda i: cot_copy(i + 1, side).wait_recv())
         for d in range(ntm):
-            frame = d * FR + f
-            block = r["hist"][d, f].astype(F32)
-            normed, inverse = norm(block)
-            for g in range(GROUPS):
-                to = slice(frame * per, (frame + 1) * per)
-                at = slice(g * BLOCK + frame * per, g * BLOCK + (frame + 1) * per)
-                mine = slice(g * per, (g + 1) * per)
-                r["xt"][g, to, :] = block[mine]
-                r["tnrm"][at, :] = normed[mine]
-                r["trinv"][at, :] = inverse[mine]
-    r["tact"][...] = r["tnrm"][...].astype(BF16)
-    r["tp"][...] = nn(r["tact"][...], r["wv"][1]).astype(BF16)
-    r["tkvt"][...] = nt(r["wt"][1], r["tact"][...]).astype(BF16)
+            for f in range(FR):
+                frame = d * FR + f
+                block = r["hcot"][d, f, mine, :].astype(F32)
+                for k, g in enumerate(groups):
+                    r["ct"][g, frame * per : (frame + 1) * per, :] = block[k * per : (k + 1) * per]
+        for g in groups:
+            rows = slice(g * BLOCK, (g + 1) * BLOCK)
+            cot = r["ct"][g].astype(BF16)
+            grad = nt(cot, r["cv"][1]).astype(BF16)
+            for h in range(HEADS):
+                r["tdos"][g, h * BLOCK : (h + 1) * BLOCK, :] = grad * r["hm"][h]
+            r["tdot"][:, rows] = nt(r["cv"][1], cot).astype(BF16)
+        for f in range(FR):
+            loop(ntm - 1, lambda i, f=f: ms_copy(f, side, i + 1).wait_recv())
+            for d in range(ntm):
+                frame = d * FR + f
+                block = r["hist"][d, f, mine, :].astype(F32)
+                normed, inverse = norm(block)
+                for k, g in enumerate(groups):
+                    to = slice(frame * per, (frame + 1) * per)
+                    at = slice(g * BLOCK + frame * per, g * BLOCK + (frame + 1) * per)
+                    piece = slice(k * per, (k + 1) * per)
+                    r["xt"][g, to, :] = block[piece]
+                    r["tnrm"][at, :] = normed[piece]
+                    r["trinv"][at, :] = inverse[piece]
+        rows = slice(side * 2 * BLOCK, (side + 1) * 2 * BLOCK)
+        r["tact"][rows, :] = r["tnrm"][rows, :].astype(BF16)
+        r["tp"][rows, :] = nn(r["tact"][rows, :], r["wv"][1]).astype(BF16)
+        r["tkvt"][:, rows] = nt(r["wt"][1], r["tact"][rows, :]).astype(BF16)
 
     def time_scores(g):
         rows = slice(g * BLOCK, (g + 1) * BLOCK)
@@ -457,42 +467,39 @@
         r["tdp"][rows, D : 2 * D] = (nn(r["tds"][g], r["tqs"][g]) * SCALE).astype(BF16)
         r["tdp"][rows, 2 * D : 3 * D] = nn(r["tprobs"][g], r["tdos"][g]).astype(BF16)
 
-    for g in range(GROUPS):
-        time_scores(g)
-    for g in range(GROUPS):
-        time_out(g)
     def mg_copy(d, side):
-        from_rows = pl.ds(side * 2 * per, 2 * per)
-        to_rows = pl.ds(pl.multiple_of(tm * part + side * 2 * per, 2 * per), 2 * per)
         return remote(
-            r["mgs"].at[d, :, from_rows, :], r["mg"].at[:, to_rows, :], r["mg_s"].at[side, d - 1],
+            r["mgs"].at[d, :, in_part(side), :], r["mg"].at[:, side_rows(tm, side), :], r["mg_s"].at[side, d - 1],
             r["mg_r"].at[side, d - 1], (lax.rem(tm + (ntm - d), ntm), sp),
         )
 
-    def mf_copy(d):
+    def mf_copy(d, side):
         return remote(
-            r["mfs"].at[d], mixed_out.at[:, own, :], r["mf_s"].at[d - 1], r["mf_r"].at[d - 1],
-            (lax.rem(tm + (ntm - d), ntm), sp),
+            r["mfs"].at[d, :, in_part(side), :], mixed_out.at[:, side_rows(tm, side), :], r["mf_s"].at[side, d - 1],
+            r["mf_r"].at[side, d - 1], (lax.rem(tm + (ntm - d), ntm), sp),
         )
 
+    def keep(side):
+        return pltpu.make_async_copy(
+            r["mfs"].at[0, :, in_part(side), :], mixed_out.at[:, side_rows(tm, side), :], r["own_sem"].at[1, side]
+        )
+
     for side in range(2):
-        for g in (2 * side, 2 * side + 1):
+        groups = (2 * side, 2 * side + 1)
+        time_inputs(side)
+        for g in groups:
+            time_scores(g)
+        for g in groups:
+            time_out(g)
+        for g in groups:
             time_grads(g)
-        for g in (2 * side, 2 * side + 1):
+        for g in groups:
             rows = slice(g * BLOCK, (g + 1) * BLOCK)
             act_grad = nt(r["tdp"][rows, :], r["wv"][1])
             r["tmix"][g] = r["ct"][g] + norm_back(act_grad, r["tnrm"][rows, :], r["trinv"][rows, :])
         ungroup(r["tmix"], r["mgs"], side)
         loop(ntm - 1, lambda i, side=side: mg_copy(i + 1, side).start())
-    r["mg"][:, own, :] = r["mgs"][0]
-
-    for g in range(GROUPS):
-        rows = slice(g * BLOCK, (g + 1) * BLOCK)
-        r["tmf"][g] = r["xt"][g] + nn(r["tatt"][rows, :], r["cv"][1])
-    for side in range(2):
-        ungroup(r["tmf"], r["mfs"], side)
-    keep = pltpu.make_async_copy(r["mfs"].at[0], mixed_out.at[:, own, :], ld.at[5])
-    keep.start()
+        r["mg"][:, side_rows(tm, side), :] = r["mgs"][0, :, side * hp : (side + 1) * hp, :]
 
     turned = r["tact"][...].astype(F32).T.astype(BF16)
     r["g0"][0:D, :] = nn(turned, r["tdp"][:, D:]).astype(BF16)
@@ -516,14 +523,17 @@
     def z_copy(a, d):
         return remote(r["zb" + str(a)].at[z], r["zb" + str(a)].at[z], r["z_s"].at[a], r["z_r"].at[a], z_peer(d))
 
+    outs = (fin0_out, fin1_out, fin2_out, fin3_out)
+
     def ag_copy(a, d):
         device, _ = plane_peer(d)
-        return remote(r["fin" + str(a)].at[my_chunk, :], r["fin" + str(a)].at[my_chunk, :], r["ag_s"].at[a], r["ag_r"].at[a], device)
+        return remote(r["fin" + str(a)], outs[a].at[my_chunk, :], r["ag_s"].at[a], r["ag_r"].at[a], device)
+
+    def fin_copy(a):
+        return pltpu.make_async_copy(r["fin" + str(a)], outs[a].at[my_chunk, :], r["out_s"].at[a])
 
     def join_copy(a):
-        return remote(
-            r["fin" + str(a)].at[my_half, :], r["fin" + str(a)].at[my_half, :], r["pg_s"].at[a], r["pg_r"].at[a], (tm, partner)
-        )
+        return remote(outs[a].at[my_half, :], outs[a].at[my_half, :], r["pg_s"].at[a], r["pg_r"].at[a], (tm, partner))
 
     def drain(ref, sem):
         pltpu.make_async_copy(ref, ref, sem).wait()
@@ -531,6 +541,8 @@
     def reduce_pair(a):
         pair_copy(a).wait_recv()
         r["h" + str(a)][...] = (r["g" + str(a)][my_half, :].astype(F32) + r["pr" + str(a)][...].astype(F32)).astype(BF16)
+
+    def reduce_plane(a):
         loop(npl - 1, lambda i: rs_copy(a, i + 1).start())
 
     def reduce_middle(a):
@@ -546,57 +558,60 @@
         total = r["zb" + str(a)][0].astype(F32)
         for k in range(1, nz):
             total = total + r["zb" + str(a)][k].astype(F32)
-        r["fin" + str(a)][my_chunk, :] = total.astype(BF16)
+        r["fin" + str(a)][...] = total.astype(BF16)
+        fin_copy(a).start()
         loop(npl - 1, lambda i: ag_copy(a, i + 1).start())
 
     def reduce_join(a):
-        drain(r["fin" + str(a)].at[0 : (npl - 1) * chunk, :], r["ag_r"].at[a])
+        fin_copy(a).wait()
+        drain(outs[a].at[0 : (npl - 1) * chunk, :], r["ag_r"].at[a])
         join_copy(a).start()
-
-    def fin_copy(a):
-        return pltpu.make_async_copy(r["fin" + str(a)], (fin0_out, fin1_out, fin2_out, fin3_out)[a], r["out_s"].at[a])
 
     def reduce_end(a):
         join_copy(a).wait_recv()
-        fin_copy(a).start()
 
     def reduce_drain(a):
         pair_copy(a).wait_send()
         drain(r["rs" + str(a)], r["rs_s"].at[a])
         drain(r["zb" + str(a)].at[0 : nz - 1], r["z_s"].at[a])
-        drain(r["fin" + str(a)].at[0 : (npl - 1) * chunk, :], r["ag_s"].at[a])
+        drain(outs[a].at[0 : (npl - 1) * chunk, :], r["ag_s"].at[a])
         join_copy(a).wait_send()
 
     pair_copy(0).start()
 
     r["dkv"][...] = jnp.zeros_like(r["dkv"])
 
+    for g in range(GROUPS):
+        rows = slice(g * BLOCK, (g + 1) * BLOCK)
+        r["tmf"][g] = r["xt"][g] + nn(r["tatt"][rows, :], r["cv"][1])
+    for side in range(2):
+        ungroup(r["tmf"], r["mfs"], side)
+        keep(side).start()
+    for f in range(FR):
+        for slot in range(3):
+            r["act_t"][f, :, slot * ROWS : (slot + 1) * ROWS] = r["act"][slot, f].astype(F32).T.astype(BF16)
+
     def mg_arrival(d, side):
-        rows = pl.ds(pl.multiple_of(lax.rem(tm + d, ntm) * part + side * 2 * per, 2 * per), 2 * per)
-        from_rows = pl.ds(side * 2 * per, 2 * per)
         return remote(
-            r["mgs"].at[d, :, from_rows, :], r["mg"].at[:, rows, :], r["mg_s"].at[side, d - 1],
-            r["mg_r"].at[side, d - 1], (tm, sp),
+            r["mgs"].at[d, :, in_part(side), :], r["mg"].at[:, side_rows(lax.rem(tm + d, ntm), side), :],
+            r["mg_s"].at[side, d - 1], r["mg_r"].at[side, d - 1], (tm, sp),
         )
 
-    for side in range(2):
-        loop(ntm - 1, lambda i, side=side: mg_arrival(i + 1, side).wait_recv())
-
-    outward = nn(r["otb"][:, 0:ROWS], r["mg"][0]) + nn(r["otb"][:, ROWS:], r["mg"][1])
-    r["g2"][0:D, :] = outward[:, 0:BLOCK].astype(BF16)
-    r["g2"][D:, :] = outward[:, BLOCK:].astype(BF16)
-    pair_copy(2).start()
+    def grads_in(j):
+        loop(ntm - 1, lambda k: mg_arrival(k + 1, j).wait_recv())
+        for f in range(FR):
+            i = 2 * f + j
+            turned = nt(r["cv"][0], r["mg"][f, j * BLOCK : (j + 1) * BLOCK, :])
+            share = jnp.broadcast_to(r["share"][i][:, None, :], (HEADS, HD, BLOCK)).reshape(D, BLOCK)
+            turned = turned * share
+            r["delta"][i] = head_sums(r["ot"][i] * turned.astype(BF16).astype(F32))
+            grad = turned.T.astype(BF16)
+            for h in range(HEADS):
+                r["dos"][i, h * BLOCK : (h + 1) * BLOCK, :] = grad * r["hm"][h]
+
+    grads_in(0)
     reduce_pair(0)
-
-    for i in range(4):
-        f, j = i // 2, i % 2
-        turned = nt(r["cv"][0], r["mg"][f, j * BLOCK : (j + 1) * BLOCK, :])
-        share = jnp.broadcast_to(r["share"][i][:, None, :], (HEADS, HD, BLOCK)).reshape(D, BLOCK)
-        turned = turned * share
-        r["delta"][i] = head_sums(r["ot"][i] * turned.astype(BF16).astype(F32))
-        grad = turned.T.astype(BF16)
-        for h in range(HEADS):
-            r["dos"][i, h * BLOCK : (h + 1) * BLOCK, :] = grad * r["hm"][h]
+    reduce_plane(0)
 
     def edge_copy(f, side):
         return remote(
@@ -604,15 +619,15 @@
             (tm, right if side else left),
         )
 
-    def edge_send(f):
+    def edge_make(f):
         for side in range(2):
             rows = slice(2 * ROWS * side, 2 * ROWS * side + ROWS)
             r["eg"][f, side] = nt(r["dkvb"][f, rows, :], r["wv"][0, :, D:]).astype(BF16)
-            edge_copy(f, side).start()
-
-    def backward_block(i):
-        f = lax.div(i, 2)
-        j = lax.rem(i, 2)
+
+    def backward_block(o):
+        f = lax.rem(o, FR)
+        j = lax.div(o, FR)
+        i = 2 * f + j
         rows = key_rows(j)
         mine = pl.ds(pl.multiple_of(j * BLOCK, BLOCK), BLOCK)
         delta = r["delta"][i]
@@ -623,6 +638,7 @@
             r["s"][pair] = nt(r["kv"][f, rows, D:], r["dos"][i, cols, :])
 
         grads(0)
+        r["dkv"][f, rows, D:] += nn(r["probs"][i], r["dos"][i])
         for pair in range(HEADS // 2):
             cols = slice(pair * 2 * BLOCK, (pair + 1) * 2 * BLOCK)
             s = r["s"].at[pair]
@@ -635,22 +651,26 @@
             outs.append(diag(nn(r["kt"][f, pair * 2 * HD : (pair + 1) * 2 * HD, rows], r["ds"][:, cols])))
         r["dq"][f, mine, :] = (jnp.concatenate(outs, axis=0) * SCALE).T.astype(BF16)
         r["dkv"][f, rows, 0:D] += nn(r["ds"][...], r["qs"][i]) * SCALE
-        r["dkv"][f, rows, D:] += nn(r["probs"][i], r["dos"][i])
-
-        @pl.when(i == 0)
+
+        @pl.when(o == 1)
         def _():
-            reduce_pair(2)
-
-        @pl.when(i == 1)
-        def _():
-            r["dkvb"][0] = r["dkv"][0].astype(BF16)
-            edge_send(0)
-            loop(ntm - 1, lambda k: mf_copy(k + 1).start())
-
-        @pl.when(i == 2)
+            grads_in(1)
+            outward = nn(r["otb"][:, 0:ROWS], r["mg"][0]) + nn(r["otb"][:, ROWS:], r["mg"][1])
+            r["g2"][0:D, :] = outward[:, 0:BLOCK].astype(BF16)
+            r["g2"][D:, :] = outward[:, BLOCK:].astype(BF16)
+            pair_copy(2).start()
+
+        @pl.when(o == 2)
         def _():
             reduce_middle(0)
-            reduce_middle(2)
+            reduce_pair(2)
+            reduce_plane(2)
+            r["dkvb"][0] = r["dkv"][0].astype(BF16)
+            edge_make(0)
+            for side in range(2):
+                edge_copy(0, side).start()
+            for side in range(2):
+                loop(ntm - 1, lambda k, side=side: mf_copy(k + 1, side).start())
 
     loop(4, backward_block)
 
@@ -664,14 +684,19 @@
     r["g1"][D:, :] = inward[:, D:].astype(BF16)
     pair_copy(1).start()
     reduce_pair(3)
+    reduce_plane(3)
     reduce_pair(1)
-    edge_send(1)
+    reduce_plane(1)
+    edge_make(1)
     for f in range(FR):
         r["fgw"][f] = nt(r["dq"][f], r["wv"][0, :, 0:D]) + nt(r["dkvb"][f, ROWS : 2 * ROWS, :], r["wv"][0, :, D:])
+    reduce_middle(2)
     reduce_share(0)
-    reduce_share(2)
     reduce_middle(3)
     reduce_middle(1)
+    reduce_share(2)
+    for side in range(2):
+        edge_copy(1, side).start()
     reduce_share(3)
     reduce_share(1)
     for a in (0, 2):
@@ -685,18 +710,21 @@
     field_copy = pltpu.make_async_copy(r["fg"], fg_out, r["out_s"].at[4])
     field_copy.start()
 
-    def mf_arrival(d):
-        rows = pl.ds(pl.multiple_of(lax.rem(tm + d, ntm) * part, part), part)
-        return remote(r["mfs"].at[d], mixed_out.at[:, rows, :], r["mf_s"].at[d - 1], r["mf_r"].at[d - 1], (tm, sp))
-
-    keep.wait()
-    loop(ntm - 1, lambda i: mf_arrival(i + 1).wait_recv())
-    loop(ntm - 1, lambda i: mf_copy(i + 1).wait_send())
+    def mf_arrival(d, side):
+        return remote(
+            r["mfs"].at[d, :, in_part(side), :], mixed_out.at[:, side_rows(lax.rem(tm + d, ntm), side), :],
+            r["mf_s"].at[side, d - 1], r["mf_r"].at[side, d - 1], (tm, sp),
+        )
+
     for side in range(2):
+        keep(side).wait()
+        loop(ntm - 1, lambda i, side=side: mf_arrival(i + 1, side).wait_recv())
+        loop(ntm - 1, lambda i, side=side: mf_copy(i + 1, side).wait_send())
         loop(ntm - 1, lambda i, side=side: mg_copy(i + 1, side).wait_send())
-    loop(ntm - 1, lambda i: cot_copy(i + 1).wait_send())
+        loop(ntm - 1, lambda i, side=side: cot_copy(i + 1, side).wait_send())
     for f in range(FR):
-        loop(ntm - 1, lambda i, f=f: ms_copy(f, i + 1).wait_send())
+        for side in range(2):
+            loop(ntm - 1, lambda i, f=f, side=side: ms_copy(f, side, i + 1).wait_send())
         for side in range(2):
             edge_copy(f, side).wait_send()
         for item in halos(f):
@@ -713,34 +741,57 @@
     reduce_drain(3)
     reduce_drain(1)
     field_copy.wait()
-    for a in range(4):
-        fin_copy(a).wait()
-
-
-def finish_kernel(factor, mixed, field, fin0, fin1, fin2, fin3, mixed_out, field_out, project_out, combine_out):
-    mixed_out[...] = mixed[...]
-    field_out[...] = field[...]
-    project_out[1, :, D:] = fin0[0:D, :].astype(F32) * factor
-    project_out[1, :, 0:D] = fin0[D:, 0:D].astype(F32) * factor
-    combine_out[1] = fin0[D:, D:].astype(F32) * factor
-    project_out[0, :, 0:BLOCK] = fin3[0:D, :].astype(F32) * factor
-    project_out[0, :, BLOCK:D] = fin3[D:, :].astype(F32) * factor
-    project_out[0, :, D : 2 * D] = fin1[0:D, :].astype(F32) * factor
-    project_out[0, :, 2 * D :] = fin1[D:, :].astype(F32) * factor
-    combine_out[0, :, 0:BLOCK] = fin2[0:D, :].astype(F32) * factor
-    combine_out[0, :, BLOCK:] = fin2[D:, :].astype(F32) * factor
+
+
+def finish_kernel(factor, *refs):
+    ins, outs = refs[:6], refs[6:10]
+    held, made = refs[10:16], refs[16:18]
+    in_sem, out_sem = refs[18:20]
+    loads = [pltpu.make_async_copy(src, dst, in_sem.at[i]) for i, (src, dst) in enumerate(zip(ins, held))]
+    order = (2, 4, 3, 5, 0, 1)
+    for i in order:
+        loads[i].start()
+    fin0, fin1, fin2, fin3 = held[2:6]
+    project, combine = made
+    stores = [
+        pltpu.make_async_copy(project.at[1], outs[2].at[1], out_sem.at[0]),
+        pltpu.make_async_copy(combine, outs[3], out_sem.at[1]),
+        pltpu.make_async_copy(project.at[0], outs[2].at[0], out_sem.at[2]),
+        pltpu.make_async_copy(held[0], outs[0], out_sem.at[3]),
+        pltpu.make_async_copy(held[1], outs[1], out_sem.at[4]),
+    ]
+    loads[2].wait()
+    project[1, :, D:] = fin0[0:D, :].astype(F32) * factor
+    project[1, :, 0:D] = fin0[D:, 0:D].astype(F32) * factor
+    stores[0].start()
+    combine[1] = fin0[D:, D:].astype(F32) * factor
+    loads[4].wait()
+    combine[0, :, 0:BLOCK] = fin2[0:D, :].astype(F32) * factor
+    combine[0, :, BLOCK:] = fin2[D:, :].astype(F32) * factor
+    stores[1].start()
+    loads[3].wait()
+    project[0, :, D : 2 * D] = fin1[0:D, :].astype(F32) * factor
+    project[0, :, 2 * D :] = fin1[D:, :].astype(F32) * factor
+    loads[5].wait()
+    project[0, :, 0:BLOCK] = fin3[0:D, :].astype(F32) * factor
+    project[0, :, BLOCK:D] = fin3[D:, :].astype(F32) * factor
+    stores[2].start()
+    for i in range(2):
+        loads[i].wait()
+        stores[3 + i].start()
+    for item in stores:
+        item.wait()
 
 
 def per_device(ntm, nsp, wave_field, cotangent, block_lists, project_weights, combine_weights):
     shapes = scratch_shapes(ntm, nsp)
     names = tuple(shapes)
     anywhere = pl.BlockSpec(memory_space=pl.ANY)
-    vmem = pl.BlockSpec(memory_space=pltpu.VMEM)
     rows = jax.ShapeDtypeStruct((FR, ROWS, D), BF16)
     results = pl.pallas_call(
         functools.partial(step_kernel, ntm, nsp, names),
         out_shape=(rows, rows) + tuple(jax.ShapeDtypeStruct((512, lanes), BF16) for lanes in LANES),
-        in_specs=[pl.BlockSpec(memory_space=pltpu.SMEM), anywhere, anywhere, anywhere, anywhere],
+        in_specs=[anywhere] * 5,
         out_specs=(anywhere,) * 6,
         scratch_shapes=list(shapes.values()),
         compiler_params=pltpu.CompilerParams(
@@ -757,8 +808,17 @@
             jax.ShapeDtypeStruct((2, D, 3 * D), F32),
             jax.ShapeDtypeStruct((2, D, D), F32),
         ),
-        in_specs=[vmem] * 6,
-        out_specs=(vmem,) * 4,
+        in_specs=[anywhere] * 6,
+        out_specs=(anywhere,) * 4,
+        scratch_shapes=[pltpu.VMEM((FR, ROWS, D), BF16)] * 2
+        + [pltpu.VMEM((512, lanes), BF16) for lanes in LANES]
+        + [
+            pltpu.VMEM((2, D, 3 * D), F32),
+            pltpu.VMEM((2, D, D), F32),
+            pltpu.SemaphoreType.DMA((6,)),
+            pltpu.SemaphoreType.DMA((5,)),
+        ],
+        compiler_params=pltpu.CompilerParams(vmem_limit_bytes=LIMIT),
         name="finish",
     )(*results)
 

time: 72.4 us -> 70.2 us (0.970)
  Pallas kernels: 71.6 us -> 69.4 us
    pallas_call x1, Pallas kernels: 68.8 us -> 66.7 us  [per_device(): pl.pallas_call(functools.partial(step_kernel, ntm, nsp, names), out_shape...]
where the time goes in v4:
time: 70.2 us; the launch traced here: 70 us
  Pallas kernels  69.4 us (99%)
    pallas_call x1, Pallas kernels, per_device(): pl.pallas_call(functools.partial(step_kernel, ntm, nsp, names), out_shape...  66.7 us
    pallas_call x1, Pallas kernels, per_device(): pl.pallas_call(functools.partial(finish_kernel, factor), out_shape=(rows,...  2.68 us

profile of v4, /device:TPU:1, one launch (start us, length us, event | category | flops | bytes accessed | tf_op | source)
XLA Modules:
  0.0 70.0 jit_solution(10226712734643234803)
XLA Ops:
  0.6 66.7 %cuboid_step.1 = (bf16[2,256,256]{2,1,0:T(8,128)(2,1)}, bf16[2,256,256]{2,1,0:T(8,128)(2,1)}, bf16[512,512]{1,0:T(8,128)(2,1)}, bf16[512,256]{1,0:T(8,128)(2,1)}...) custom-call(s32[2,2,4]{2,1,0:T(2,128)} %lists_hbm.1, bf16[2,256,256]{2,1,0:T(8,128)(2,1)} %x_hbm.1, ...), custom_call_target="tpu_custom_call" | custom-call | tf_op jit(solution)/shard_map/cuboid_step/pallas_call | solution.py:791
  67.4 2.7 %finish.1 = (bf16[2,256,256]{2,1,0:T(8,128)(2,1)}, bf16[2,256,256]{2,1,0:T(8,128)(2,1)}, f32[2,256,768]{2,1,0:T(8,128)}, f32[2,256,256]{2,1,0:T(8,128)}) custom-call(bf16[2,256,256]{2,1,0:T(8,128)(2,1)} %get-tuple-element.10.refs_0_, bf16[2,256,256]{2,1,0:T(8,128)(2,1)} %get-tuple-element.11.refs_1_, bf16[512,512]{1,0:T(8,128)(2,1)} %get-tuple-element.12.refs_2_, ...), custom_call_target="tpu_custom_call" | custom-call | tf_op jit(solution)/shard_map/finish/pallas_call | solution.py:803

commit v5 on v4

--- a/solution.py
+++ b/solution.py
@@ -609,9 +609,11 @@
             for h in range(HEADS):
                 r["dos"][i, h * BLOCK : (h + 1) * BLOCK, :] = grad * r["hm"][h]
 
-    grads_in(0)
     reduce_pair(0)
     reduce_plane(0)
+    for side in range(2):
+        loop(ntm - 1, lambda k, side=side: mf_copy(k + 1, side).start())
+    grads_in(0)
 
     def edge_copy(f, side):
         return remote(
@@ -669,8 +671,6 @@
             edge_make(0)
             for side in range(2):
                 edge_copy(0, side).start()
-            for side in range(2):
-                loop(ntm - 1, lambda k, side=side: mf_copy(k + 1, side).start())
 
     loop(4, backward_block)
 

time: 70.2 us -> 68 us (0.969)
  Pallas kernels: 69.4 us -> 67.2 us
    pallas_call x1, Pallas kernels: 66.7 us -> 64.5 us  [per_device(): pl.pallas_call(functools.partial(step_kernel, ntm, nsp, names), out_shape...]
where the time goes in v5:
time: 68 us; the launch traced here: 67.8 us
  Pallas kernels  67.2 us (99%)
    pallas_call x1, Pallas kernels, per_device(): pl.pallas_call(functools.partial(step_kernel, ntm, nsp, names), out_shape...  64.5 us
    pallas_call x1, Pallas kernels, per_device(): pl.pallas_call(functools.partial(finish_kernel, factor), out_shape=(rows,...  2.68 us

profile of v5, /device:TPU:1, one launch (start us, length us, event | category | flops | bytes accessed | tf_op | source)
XLA Modules:
  0.0 67.8 jit_solution(8689068995896347188)
XLA Ops:
  0.6 64.5 %cuboid_step.1 = (bf16[2,256,256]{2,1,0:T(8,128)(2,1)}, bf16[2,256,256]{2,1,0:T(8,128)(2,1)}, bf16[512,512]{1,0:T(8,128)(2,1)}, bf16[512,256]{1,0:T(8,128)(2,1)}...) custom-call(s32[2,2,4]{2,1,0:T(2,128)} %lists_hbm.1, bf16[2,256,256]{2,1,0:T(8,128)(2,1)} %x_hbm.1, ...), custom_call_target="tpu_custom_call" | custom-call | tf_op jit(solution)/shard_map/cuboid_step/pallas_call | solution.py:791
  65.2 2.7 %finish.1 = (bf16[2,256,256]{2,1,0:T(8,128)(2,1)}, bf16[2,256,256]{2,1,0:T(8,128)(2,1)}, f32[2,256,768]{2,1,0:T(8,128)}, f32[2,256,256]{2,1,0:T(8,128)}) custom-call(bf16[2,256,256]{2,1,0:T(8,128)(2,1)} %get-tuple-element.10.refs_0_, bf16[2,256,256]{2,1,0:T(8,128)(2,1)} %get-tuple-element.11.refs_1_, bf16[512,512]{1,0:T(8,128)(2,1)} %get-tuple-element.12.refs_2_, ...), custom_call_target="tpu_custom_call" | custom-call | tf_op jit(solution)/shard_map/finish/pallas_call | solution.py:803

commit v6 on v5

--- a/solution.py
+++ b/solution.py
@@ -158,6 +158,8 @@
         rs_r=dma((4,)),
         z_s=dma((4,)),
         z_r=dma((4,)),
+        col_s=dma((1,)),
+        col_r=dma((1,)),
         ag_s=dma((4,)),
         ag_r=dma((4,)),
     )
@@ -529,6 +531,42 @@
         device, _ = plane_peer(d)
         return remote(r["fin" + str(a)], outs[a].at[my_chunk, :], r["ag_s"].at[a], r["ag_r"].at[a], device)
 
+    along = lax.rem(place, 4)
+    line = lax.div(place, 4)
+    lines = npl // 4
+    my_line = pl.ds(pl.multiple_of(core * 256 + line * 4 * chunk, 4 * chunk), 4 * chunk)
+
+    def place_device(other):
+        return (lax.div(other, 2), z * CORES + lax.rem(other, 2) * 2 + core)
+
+    def row_copy(d):
+        device = place_device(line * 4 + lax.rem(along + d, 4))
+        return remote(r["fin0"], outs[0].at[my_chunk, :], r["ag_s"].at[0], r["ag_r"].at[0], device)
+
+    def col_copy(d):
+        device = place_device(lax.rem(line + d, lines) * 4 + along)
+        return remote(
+            outs[0].at[my_line, :], outs[0].at[my_line, :], r["col_s"].at[0], r["col_r"].at[0], device
+        )
+
+    def share_rows():
+        drain(r["zb0"].at[0 : nz - 1], r["z_r"].at[0])
+        total = r["zb0"][0].astype(F32)
+        for k in range(1, nz):
+            total = total + r["zb0"][k].astype(F32)
+        r["fin0"][...] = total.astype(BF16)
+        fin_copy(0).start()
+        loop(3, lambda i: row_copy(i + 1).start())
+
+    def share_columns():
+        fin_copy(0).wait()
+        drain(outs[0].at[0 : 3 * chunk, :], r["ag_r"].at[0])
+        loop(lines - 1, lambda i: col_copy(i + 1).start())
+
+    def join_columns():
+        drain(outs[0].at[0 : (lines - 1) * 4 * chunk, :], r["col_r"].at[0])
+        join_copy(0).start()
+
     def fin_copy(a):
         return pltpu.make_async_copy(r["fin" + str(a)], outs[a].at[my_chunk, :], r["out_s"].at[a])
 
@@ -574,7 +612,11 @@
         pair_copy(a).wait_send()
         drain(r["rs" + str(a)], r["rs_s"].at[a])
         drain(r["zb" + str(a)].at[0 : nz - 1], r["z_s"].at[a])
-        drain(outs[a].at[0 : (npl - 1) * chunk, :], r["ag_s"].at[a])
+        if a == 0:
+            drain(outs[0].at[0 : 3 * chunk, :], r["ag_s"].at[0])
+            drain(outs[0].at[0 : (lines - 1) * 4 * chunk, :], r["col_s"].at[0])
+        else:
+            drain(outs[a].at[0 : (npl - 1) * chunk, :], r["ag_s"].at[a])
         join_copy(a).wait_send()
 
     pair_copy(0).start()
@@ -691,16 +733,17 @@
     for f in range(FR):
         r["fgw"][f] = nt(r["dq"][f], r["wv"][0, :, 0:D]) + nt(r["dkvb"][f, ROWS : 2 * ROWS, :], r["wv"][0, :, D:])
     reduce_middle(2)
-    reduce_share(0)
+    share_rows()
     reduce_middle(3)
     reduce_middle(1)
+    share_columns()
     reduce_share(2)
     for side in range(2):
         edge_copy(1, side).start()
     reduce_share(3)
     reduce_share(1)
-    for a in (0, 2):
-        reduce_join(a)
+    join_columns()
+    reduce_join(2)
 
     for f in range(FR):
         for side in range(2):

time: 68 us -> 67.8 us (level)
  no operation moved by 1% of the time
where the time goes in v6:
time: 67.8 us; the launch traced here: 67.7 us
  Pallas kernels  67 us (99%)
    pallas_call x1, Pallas kernels, per_device(): pl.pallas_call(functools.partial(step_kernel, ntm, nsp, names), out_shape...  64.4 us
    pallas_call x1, Pallas kernels, per_device(): pl.pallas_call(functools.partial(finish_kernel, factor), out_shape=(rows,...  2.68 us

profile of v6, /device:TPU:1, one launch (start us, length us, event | category | flops | bytes accessed | tf_op | source)
XLA Modules:
  0.0 67.7 jit_solution(6861275722324827176)
XLA Ops:
  0.6 64.4 %cuboid_step.1 = (bf16[2,256,256]{2,1,0:T(8,128)(2,1)}, bf16[2,256,256]{2,1,0:T(8,128)(2,1)}, bf16[512,512]{1,0:T(8,128)(2,1)}, bf16[512,256]{1,0:T(8,128)(2,1)}...) custom-call(s32[2,2,4]{2,1,0:T(2,128)} %lists_hbm.1, bf16[2,256,256]{2,1,0:T(8,128)(2,1)} %x_hbm.1, ...), custom_call_target="tpu_custom_call" | custom-call | tf_op jit(solution)/shard_map/cuboid_step/pallas_call | solution.py:834
  65.0 2.7 %finish.1 = (bf16[2,256,256]{2,1,0:T(8,128)(2,1)}, bf16[2,256,256]{2,1,0:T(8,128)(2,1)}, f32[2,256,768]{2,1,0:T(8,128)}, f32[2,256,256]{2,1,0:T(8,128)}) custom-call(bf16[2,256,256]{2,1,0:T(8,128)(2,1)} %get-tuple-element.10.refs_0_, bf16[2,256,256]{2,1,0:T(8,128)(2,1)} %get-tuple-element.11.refs_1_, bf16[512,512]{1,0:T(8,128)(2,1)} %get-tuple-element.12.refs_2_, ...), custom_call_target="tpu_custom_call" | custom-call | tf_op jit(solution)/shard_map/finish/pallas_call | solution.py:846
